TPU v7x, 32 devices: a whole 2x2x4 slice. The times are simulated.
32 devices in a mesh: dp: 16 (over z, x, core), tensor: 2 (over y).
Axes of the slice: x: 2, y: 2, z: 4, core: 2. Of those that a mesh axis runs over, the one named last changes fastest.
Arguments:
- block_input: bfloat16 [8192, 1024], P(('dp', 'tensor')), may hold values from -6 to 6
- cotangent: bfloat16 [8192, 1024], P(('dp', 'tensor')), may hold values from -6 to 6
- segment_ids: int32 [16, 512], P('dp'), may hold values from 0 to 2, never falling along the last dimension, each value on 1 to 384 neighbouring positions
- positions: int32 [16, 512], P('dp'), may hold values from 0 to 8191
- norm_gains: bfloat16 [2, 1024], P(None, 'dp'), may hold values from 0.25 to 1.75
- qk_gains: bfloat16 [2, 64], P(None, 'dp'), may hold values from 0.6 to 1.6
- w_query: bfloat16 [1024, 1024], P('dp', 'tensor'), may hold values from -0.1875 to 0.1875
- w_keyval: bfloat16 [2, 1024, 512], P(None, 'dp', 'tensor'), may hold values from -0.1875 to 0.1875
- w_output: bfloat16 [1024, 1024], P('tensor', 'dp'), may hold values from -0.75 to 0.75
- w_gate_up: bfloat16 [2, 1024, 4608], P(None, 'dp', 'tensor'), may hold values from -0.1875 to 0.1875
- w_down: bfloat16 [4608, 1024], P('tensor', 'dp'), may hold values from -0.09375 to 0.09375
Outputs:
- block_output: bfloat16 [8192, 1024], P(('dp', 'tensor'))
- grad_input: float32 [8192, 1024], P(('dp', 'tensor'))
- grad_norm_gains: float32 [2, 1024], P(None, 'dp')
- grad_qk_gains: float32 [2, 64], P(None, 'dp')
- grad_query: float32 [1024, 1024], P('dp', 'tensor')
- grad_keyval: float32 [2, 1024, 512], P(None, 'dp', 'tensor')
- grad_output: float32 [1024, 1024], P('tensor', 'dp')
- grad_gate_up: float32 [2, 1024, 4608], P(None, 'dp', 'tensor')
- grad_down: float32 [4608, 1024], P('tensor', 'dp')
Inputs may be any that keep to these rules, and one draw needn't show every extreme that they name: `segment_ids`: ids never fall along a row; each document spans 1 to 384 tokens and one spans exactly that many.
All inputs are finite; a program needn't handle non-finite values.
Results may differ from a plain program's by a relative error of at most 0.028.
Values may be sent and summed in bfloat16 or wider, within the bound.
A program may use at most 128 MiB of HBM per device.

v0:
```python
import math

import jax
import jax.numpy as jnp
from jax import lax
from jax.sharding import PartitionSpec as P

HD = 64


EPSILON = 1e-05
ROPE_BASE = 1000000.0
NEG_FILL = -1e30


def rms_forward(values, gain):
    scale = lax.rsqrt(jnp.mean(values * values, axis=-1, keepdims=True) + EPSILON)
    return (values * scale * gain, scale)


def rms_backward(values, scale, gain, grad):
    weighted = grad * gain
    inner = jnp.mean(weighted * values, axis=-1, keepdims=True)
    return scale * (weighted - values * scale * scale * inner)


def rope_tables(places):
    freqs = ROPE_BASE ** (-jnp.arange(0, HD, 2).astype(jnp.float32) / HD)
    angles = places.astype(jnp.float32)[..., None] * freqs
    angles = jnp.concatenate([angles, angles], axis=-1)
    return (jnp.cos(angles), jnp.sin(angles))


def rotate_half(values):
    half = values.shape[-1] // 2
    return jnp.concatenate([-values[..., half:], values[..., :half]], axis=-1)


def rotate_back(values):
    half = values.shape[-1] // 2
    return jnp.concatenate([values[..., half:], -values[..., :half]], axis=-1)


def allowed_mask(segs):
    length = segs.shape[0]
    index = jnp.arange(length, dtype=jnp.int32)
    return (segs[:, None] == segs[None, :]) & (index[None, :] <= index[:, None])


def contract(left, right, left_dim, right_dim):
    return lax.dot_general(
        left, right, (((left_dim,), (right_dim,)), ((), ())), preferred_element_type=jnp.float32
    )


def fdot(left, right):
    return jnp.dot(left, right, preferred_element_type=jnp.float32)


def row_scores(q_rot, k_rot):
    kv_heads = k_rot.shape[1]
    groups = q_rot.shape[1] // kv_heads
    q_four = q_rot.reshape(q_rot.shape[0], kv_heads, groups, HD)
    scores = jnp.einsum("ikgd,jkd->kgij", q_four, k_rot, preferred_element_type=jnp.float32)
    return (scores / math.sqrt(HD), q_four)


def attend_row(q_rot, k_rot, values, segs):
    scores, q_four = row_scores(q_rot, k_rot)
    allowed = allowed_mask(segs)[None, None]
    masked = jnp.where(allowed, scores, NEG_FILL)
    top = jnp.max(masked, axis=-1, keepdims=True)
    expd = jnp.where(allowed, jnp.exp(masked - top), 0.0)
    total = jnp.sum(expd, axis=-1, keepdims=True)
    probs = (expd / total).astype(jnp.bfloat16)
    log_total = top[..., 0] + jnp.log(total[..., 0])
    attended = jnp.einsum("kgij,jkd->ikgd", probs, values, preferred_element_type=jnp.float32)
    return (attended.reshape(q_rot.shape).astype(jnp.bfloat16), log_total)


def back_row(q_rot, k_rot, values, grad_att, log_total, segs):
    scores, q_four = row_scores(q_rot, k_rot)
    allowed = allowed_mask(segs)[None, None]
    masked = jnp.where(allowed, scores, NEG_FILL)
    probs = jnp.where(allowed, jnp.exp(masked - log_total[..., None]), 0.0)
    probs_b = probs.astype(jnp.bfloat16)
    grad_four = grad_att.reshape(q_four.shape)
    grad_values = jnp.einsum(
        "kgij,ikgd->jkd", probs_b, grad_four, preferred_element_type=jnp.float32
    )
    grad_p = jnp.einsum("ikgd,jkd->kgij", grad_four, values, preferred_element_type=jnp.float32)
    delta = jnp.sum(probs * grad_p, axis=-1, keepdims=True)
    d_scores = (probs * (grad_p - delta) / math.sqrt(HD)).astype(jnp.bfloat16)
    grad_q = jnp.einsum(
        "kgij,jkd->ikgd", d_scores, k_rot, preferred_element_type=jnp.float32
    ).reshape(q_rot.shape)
    grad_k = jnp.einsum("kgij,ikgd->jkd", d_scores, q_four, preferred_element_type=jnp.float32)
    return (grad_q, grad_k, grad_values)


def collect(values):
    return lax.all_gather(values, "tensor", axis=0, tiled=True)


def spread(values):
    return lax.psum_scatter(values, "tensor", scatter_dimension=0, tiled=True)


def on_device(
    block_input,
    cotangent,
    segment_ids,
    positions,
    norm_gains,
    qk_gains,
    w_query,
    w_keyval,
    w_output,
    w_gate_up,
    w_down,
):
    rows_here, row_len = segment_ids.shape
    tokens_here = rows_here * row_len
    query_full, keyval_full, output_full, norm_full, qk_full = (
        lax.all_gather(w_query, "dp", axis=0, tiled=True),
        lax.all_gather(w_keyval, "dp", axis=1, tiled=True),
        lax.all_gather(w_output, "dp", axis=1, tiled=True),
        lax.all_gather(norm_gains, "dp", axis=1, tiled=True),
        lax.all_gather(qk_gains, "dp", axis=1, tiled=True),
    )
    heads_here = query_full.shape[1] // HD
    kv_here = keyval_full.shape[2] // HD
    gain_attn = norm_full[0].astype(jnp.float32)
    gain_ffn = norm_full[1].astype(jnp.float32)
    gain_q = qk_full[0].astype(jnp.float32)
    gain_k = qk_full[1].astype(jnp.float32)
    xlocal = block_input.astype(jnp.float32)
    normed_f, scale1 = rms_forward(xlocal, gain_attn)
    normed1 = collect(normed_f.astype(jnp.bfloat16))
    query = fdot(normed1, query_full).reshape(rows_here, row_len, heads_here, HD)
    keys = fdot(normed1, keyval_full[0]).reshape(rows_here, row_len, kv_here, HD)
    values = (
        fdot(normed1, keyval_full[1]).astype(jnp.bfloat16).reshape(rows_here, row_len, kv_here, HD)
    )
    q_norm, q_scale = rms_forward(query, gain_q)
    k_norm, k_scale = rms_forward(keys, gain_k)
    cosv, sinv = rope_tables(positions)
    cosv = cosv[:, :, None, :]
    sinv = sinv[:, :, None, :]
    q_rot = (q_norm * cosv + rotate_half(q_norm) * sinv).astype(jnp.bfloat16)
    k_rot = (k_norm * cosv + rotate_half(k_norm) * sinv).astype(jnp.bfloat16)
    attended, log_total = jax.vmap(attend_row)(q_rot, k_rot, values, segment_ids)
    att_flat = attended.reshape(tokens_here, heads_here * HD)
    hidden = xlocal + spread(fdot(att_flat, output_full))
    normed_g, scale2 = rms_forward(hidden, gain_ffn)
    gate_up_full, down_full = (
        lax.all_gather(w_gate_up, "dp", axis=1, tiled=True),
        lax.all_gather(w_down, "dp", axis=1, tiled=True),
    )
    normed2 = collect(normed_g.astype(jnp.bfloat16))
    gate_proj = fdot(normed2, gate_up_full[0])
    up_proj = fdot(normed2, gate_up_full[1])
    sigmoid_gate = jax.nn.sigmoid(gate_proj)
    silu_gate = gate_proj * sigmoid_gate
    act = (silu_gate * up_proj).astype(jnp.bfloat16)
    block_output = (hidden + spread(fdot(act, down_full))).astype(jnp.bfloat16)
    gate_up_full, down_full = (
        lax.all_gather(w_gate_up, "dp", axis=1, tiled=True),
        lax.all_gather(w_down, "dp", axis=1, tiled=True),
    )
    dy_rows = collect(cotangent)
    grad_act = contract(dy_rows, down_full, 1, 1)
    grad_down = contract(act, dy_rows, 0, 0)
    d_gate = (grad_act * up_proj * sigmoid_gate * (1.0 + gate_proj * (1.0 - sigmoid_gate))).astype(
        jnp.bfloat16
    )
    d_up = (grad_act * silu_gate).astype(jnp.bfloat16)
    grad_gate_up = jnp.stack([contract(normed2, d_gate, 0, 0), contract(normed2, d_up, 0, 0)])
    grad_n2 = spread(
        contract(d_gate, gate_up_full[0], 1, 1) + contract(d_up, gate_up_full[1], 1, 1)
    )
    gain_ffn_grad = jnp.sum(grad_n2 * hidden * scale2, axis=0)
    grad_hidden = cotangent.astype(jnp.float32) + rms_backward(hidden, scale2, gain_ffn, grad_n2)
    query_full, keyval_full, output_full, norm_full, qk_full = (
        lax.all_gather(w_query, "dp", axis=0, tiled=True),
        lax.all_gather(w_keyval, "dp", axis=1, tiled=True),
        lax.all_gather(w_output, "dp", axis=1, tiled=True),
        lax.all_gather(norm_gains, "dp", axis=1, tiled=True),
        lax.all_gather(qk_gains, "dp", axis=1, tiled=True),
    )
    grad_rows = collect(grad_hidden.astype(jnp.bfloat16))
    grad_att = (
        contract(grad_rows, output_full, 1, 1)
        .astype(jnp.bfloat16)
        .reshape(rows_here, row_len, heads_here, HD)
    )
    grad_out = contract(att_flat, grad_rows, 0, 0)
    grad_qrot, grad_krot, grad_vals = jax.vmap(back_row)(
        q_rot, k_rot, values, grad_att, log_total, segment_ids
    )
    grad_qn = grad_qrot * cosv + rotate_back(grad_qrot * sinv)
    grad_kn = grad_krot * cosv + rotate_back(grad_krot * sinv)
    gain_q_grad = jnp.sum(grad_qn * query * q_scale, axis=(0, 1, 2))
    gain_k_grad = jnp.sum(grad_kn * keys * k_scale, axis=(0, 1, 2))
    d_query = (
        rms_backward(query, q_scale, gain_q, grad_qn)
        .astype(jnp.bfloat16)
        .reshape(tokens_here, heads_here * HD)
    )
    d_keys = (
        rms_backward(keys, k_scale, gain_k, grad_kn)
        .astype(jnp.bfloat16)
        .reshape(tokens_here, kv_here * HD)
    )
    d_values = grad_vals.astype(jnp.bfloat16).reshape(tokens_here, kv_here * HD)
    grad_wq = contract(normed1, d_query, 0, 0)
    grad_kv = jnp.stack([contract(normed1, d_keys, 0, 0), contract(normed1, d_values, 0, 0)])
    grad_n1 = spread(
        contract(d_query, query_full, 1, 1)
        + contract(d_keys, keyval_full[0], 1, 1)
        + contract(d_values, keyval_full[1], 1, 1)
    )
    gain_attn_grad = jnp.sum(grad_n1 * xlocal * scale1, axis=0)
    grad_input = grad_hidden + rms_backward(xlocal, scale1, gain_attn, grad_n1)
    norm_terms = jnp.stack([gain_attn_grad, gain_ffn_grad])
    qk_terms = jnp.stack([gain_q_grad, gain_k_grad])
    norm_sum, qk_sum = lax.psum((norm_terms, qk_terms), "tensor")
    shard_wq, shard_kv, shard_out, shard_norm, shard_qk, shard_gate_up, shard_down = (
        lax.psum_scatter(
            grad_wq.astype(jnp.bfloat16), "dp", scatter_dimension=0, tiled=True
        ).astype(jnp.float32),
        lax.psum_scatter(
            grad_kv.astype(jnp.bfloat16), "dp", scatter_dimension=1, tiled=True
        ).astype(jnp.float32),
        lax.psum_scatter(
            grad_out.astype(jnp.bfloat16), "dp", scatter_dimension=1, tiled=True
        ).astype(jnp.float32),
        lax.psum_scatter(
            norm_sum.astype(jnp.bfloat16), "dp", scatter_dimension=1, tiled=True
        ).astype(jnp.float32),
        lax.psum_scatter(qk_sum.astype(jnp.bfloat16), "dp", scatter_dimension=1, tiled=True).astype(
            jnp.float32
        ),
        lax.psum_scatter(
            grad_gate_up.astype(jnp.bfloat16), "dp", scatter_dimension=1, tiled=True
        ).astype(jnp.float32),
        lax.psum_scatter(
            grad_down.astype(jnp.bfloat16), "dp", scatter_dimension=1, tiled=True
        ).astype(jnp.float32),
    )
    return (
        block_output,
        grad_input,
        shard_norm,
        shard_qk,
        shard_wq,
        shard_kv,
        shard_out,
        shard_gate_up,
        shard_down,
    )


def solution(mesh):
    return jax.shard_map(
        on_device,
        mesh=mesh,
        in_specs=(
            P(("dp", "tensor"), None),
            P(("dp", "tensor"), None),
            P("dp", None),
            P("dp", None),
            P(None, "dp"),
            P(None, "dp"),
            P("dp", "tensor"),
            P(None, "dp", "tensor"),
            P("tensor", "dp"),
            P(None, "dp", "tensor"),
            P("tensor", "dp"),
        ),
        out_specs=(
            P(("dp", "tensor"), None),
            P(("dp", "tensor"), None),
            P(None, "dp"),
            P(None, "dp"),
            P("dp", "tensor"),
            P(None, "dp", "tensor"),
            P("tensor", "dp"),
            P(None, "dp", "tensor"),
            P("tensor", "dp"),
        ),
        check_vma=False,
    )
```

profile of v0, /device:TPU:0, one launch (start us, length us, event | category | flops | bytes accessed | tf_op | source)
XLA Modules:
  0.0 1001.4 jit_solution(7636723697401440509)
XLA Ops:
  7.2 23.3 %all-gather = bf16[16,64,2]{1,2,0:T(2,128)(2,1)S(1)} all-gather(bf16[1,64,2]{1,2,0:T(2,128)(2,1)} %bitcast.281), channel_id=1, replica_groups=mesh['dp'=16,'tensor'=2] {'dp'}, dimensions={0}, use_global_device_ids=true | all-gather | bytes 4352 | tf_op jit(solution)/shard_map/all_gather | solution.py:128
  31.2 1.2 fusion.39
  32.4 2.0 fusion.34
  36.6 17.6 %all-gather.1 = bf16[16,4,2]{1,2,0:T(2,128)(2,1)S(1)} all-gather(bf16[1,4,2]{1,2,0:T(2,128)(2,1)} %bitcast.282), channel_id=1, replica_groups=mesh['dp'=16,'tensor'=2] {'dp'}, dimensions={0}, use_global_device_ids=true | all-gather | bytes 272 | tf_op jit(solution)/shard_map/all_gather | solution.py:129
  56.4 36.8 %all-gather.16.cloned.1.call-done = bf16[1024,512]{1,0:T(8,128)(2,1)} async-done(((bf16[64,512]{1,0:T(8,128)(2,1)}), bf16[1024,512]{1,0:T(8,128)(2,1)}) %all-gather.16.cloned.1.call-update) | async-done | bytes 1048592 | tf_op jit(solution)/shard_map/all_gather | solution.py:125
  93.2 2.3 fusion.69
  95.7 36.6 %all-gather.14.cloned.1.call-done = bf16[2,1024,256]{2,1,0:T(8,128)(2,1)} async-done(((bf16[2,64,256]{2,1,0:T(8,128)(2,1)}), bf16[2,1024,256]{2,1,0:T(8,128)(2,1)}) %all-gather.14.cloned.1.call-update) | async-done | bytes 1048592 | tf_op jit(solution)/shard_map/all_gather | solution.py:126
  132.3 1.5 fusion.58
  137.0 1.4 fusion.48
  138.4 1.5 fusion.68
  140.4 1.5 fusion.4
  141.9 1.3 copy-done
  143.4 2.2 fusion.21
  145.6 25.6 %all-gather.18.cloned.1.call-done = bf16[512,1024]{0,1:T(8,128)(2,1)} async-done(((bf16[512,64]{0,1:T(8,128)(2,1)}), bf16[512,1024]{0,1:T(8,128)(2,1)}) %all-gather.18.cloned.1.call-update) | async-done | bytes 1048592 | tf_op jit(solution)/shard_map/all_gather | solution.py:127
  171.2 3.3 fusion.70
  174.7 31.0 %reduce-scatter.14.cloned.1.call-done = f32[256,1024]{1,0:T(8,128)} async-done(((f32[512,1024]{1,0:T(8,128)}), f32[256,1024]{1,0:T(8,128)}) %reduce-scatter.14.cloned.1.call-update) | async-done | bytes 1048592 | tf_op jit(solution)/shard_map/reduce_scatter | solution.py:106
  205.6 1.4 multiply_reduce_fusion.2
  207.6 1.6 multiply_convert_fusion.3
  211.7 19.0 %all-gather.20.cloned.1.call-done = bf16[512,1024]{1,0:T(8,128)(2,1)} async-done(((bf16[256,1024]{1,0:T(8,128)(2,1)}), bf16[512,1024]{1,0:T(8,128)(2,1)}) %all-gather.20.cloned.1.call-update) | async-done | bytes 1048592 | tf_op jit(solution)/shard_map/all_gather | solution.py:102
  230.7 83.2 %all-gather.22.cloned.1.call-done = bf16[2,1024,2304]{2,1,0:T(8,128)(2,1)} async-done(((bf16[2,64,2304]{2,1,0:T(8,128)(2,1)}), bf16[2,1024,2304]{2,1,0:T(8,128)(2,1)}) %all-gather.22.cloned.1.call-update) | async-done | bytes 9437200 | tf_op jit(solution)/shard_map/all_gather | solution.py:157
  314.0 7.6 fusion.17
  321.6 4.2 fusion.19
  325.8 9.4 all-gather.26.cloned.1.call-done
  335.2 55.4 %all-gather.24.cloned.1.call-done = bf16[2304,1024]{0,1:T(8,128)(2,1)} async-done(((bf16[2304,64]{0,1:T(8,128)(2,1)}), bf16[2304,1024]{0,1:T(8,128)(2,1)}) %all-gather.24.cloned.1.call-update) | async-done | bytes 4718608 | tf_op jit(solution)/shard_map/all_gather | solution.py:158
  390.7 10.8 %multiply_convert_fusion = (bf16[512,2304]{1,0:T(8,128)(2,1)S(1)}, bf16[512,2304]{1,0:T(8,128)(2,1)S(1)}, bf16[512,2304]{1,0:T(8,128)(2,1)}) fusion(f32[512,2304]{1,0:T(8,128)} %fusion.17, f32[512,2304]{1,0:T(8,128)} %fusion.19, bf16[512,1024]{1,0:T(8,128)(2,1)} %all-gather.26.cloned.1.call-done, bf16[2304,1024]{0,1:T(8,128)(2,1)} %all-gather.24.cloned.1.call-done), kind=kOutput, calls=%fused_computation.20 | convolution fusion | flops 2433613824 | bytes 22282240 | tf_op jit(solution)/shard_map/dot_general | solution.py:51
  401.4 6.2 fusion.16
  407.7 6.4 fusion.20
  414.2 30.6 %reduce-scatter.18.cloned.1.call-done = f32[256,1024]{1,0:T(8,128)} async-done(((f32[512,1024]{1,0:T(8,128)}), f32[256,1024]{1,0:T(8,128)}) %reduce-scatter.18.cloned.1.call-update) | async-done | bytes 1048592 | tf_op jit(solution)/shard_map/reduce_scatter | solution.py:106
  444.7 2.1 multiply_reduce_fusion
  447.4 2.5 fusion.65
  450.2 1.2 mul.642
  451.4 1.3 mul.643
  452.7 1.3 log_add_fusion
  454.1 17.3 %all-gather.28.cloned.1.call-done = bf16[512,1024]{1,0:T(8,128)(2,1)} async-done(((bf16[256,1024]{1,0:T(8,128)(2,1)}), bf16[512,1024]{1,0:T(8,128)(2,1)}) %all-gather.28.cloned.1.call-update) | async-done | bytes 1048592 | tf_op jit(solution)/shard_map/all_gather | solution.py:102
  471.4 2.3 convolution_convert_fusion.7
  473.7 5.0 fusion
  479.7 2.6 fusion.10
  483.4 1.4 broadcast_multiply_fusion
  484.8 1.6 fusion.31
  488.2 1.2 fusion.46
  490.7 1.8 add_add_fusion
  492.5 1.7 convolution_convert_fusion.4
  494.3 1.4 fusion.30
  497.4 3.5 convolution_convert_fusion.3
  501.2 6.0 convolution_convert_fusion
  507.3 7.2 fusion.71
  514.6 6.1 fusion.7
  520.8 4.3 fusion.6
  525.3 1.5 fusion.42
  526.8 5.1 all-reduce.1
  532.9 8.4 pad_maximum_fusion
  543.2 43.1 %reduce-scatter.22.cloned.1.call-done = bf16[64,512]{1,0:T(8,128)(2,1)} async-done(((bf16[1024,512]{1,0:T(8,128)(2,1)}), bf16[64,512]{1,0:T(8,128)(2,1)}) %reduce-scatter.22.cloned.1.call-update) | async-done | bytes 65552 | tf_op jit(solution)/shard_map/reduce_scatter | solution.py:229
  586.3 1.5 convert_element_type.198
  587.8 59.2 %reduce-scatter.24.cloned.1.call-done = bf16[2,64,256]{2,1,0:T(8,128)(2,1)} async-done(((bf16[2,1024,256]{2,1,0:T(8,128)(2,1)}), bf16[2,64,256]{2,1,0:T(8,128)(2,1)}) %reduce-scatter.24.cloned.1.call-update) | async-done | bytes 65552 | tf_op jit(solution)/shard_map/reduce_scatter | solution.py:232
  647.0 1.5 convert_element_type.199
  648.5 58.7 %reduce-scatter.26.cloned.1.call-done = bf16[512,64]{0,1:T(8,128)(2,1)} async-done(((bf16[512,1024]{0,1:T(8,128)(2,1)}), bf16[512,64]{0,1:T(8,128)(2,1)}) %reduce-scatter.26.cloned.1.call-update) | async-done | bytes 65552 | tf_op jit(solution)/shard_map/reduce_scatter | solution.py:235
  707.2 1.5 convert_element_type.201
  708.7 76.9 %reduce-scatter.30.cloned.1.call-done = bf16[2304,64]{0,1:T(8,128)(2,1)} async-done(((bf16[2304,1024]{0,1:T(8,128)(2,1)}), bf16[2304,64]{0,1:T(8,128)(2,1)}) %reduce-scatter.30.cloned.1.call-update) | async-done | bytes 294928 | tf_op jit(solution)/shard_map/reduce_scatter | solution.py:247
  785.7 1.8 convert_element_type.204
  787.5 30.2 %all-reduce = bf16[2,64]{1,0:T(2,128)(2,1)S(1)} all-reduce(bf16[2,64]{1,0:T(2,128)(2,1)S(1)} %get-tuple-element.16), channel_id=7, replica_groups=mesh['dp'=16,'tensor'=2] {'dp'}, use_global_device_ids=true, to_apply=%region_23.24.clone | all-reduce | flops 128 | bytes 512
  818.8 3.3 fusion.38
  822.1 55.9 %reduce-scatter.32.cloned.1.call-done = bf16[64,2]{1,0:T(8,128)(2,1)} async-done(((bf16[1024,2]{1,0:T(8,128)(2,1)}), bf16[64,2]{1,0:T(8,128)(2,1)}) %reduce-scatter.32.cloned.1.call-update) | async-done | bytes 272
  879.3 112.9 %reduce-scatter.28.cloned.1.call-done = bf16[2,64,2304]{2,1,0:T(8,128)(2,1)} async-done(((bf16[2,1024,2304]{2,1,0:T(8,128)(2,1)}), bf16[2,64,2304]{2,1,0:T(8,128)(2,1)}) %reduce-scatter.28.cloned.1.call-update) | async-done | bytes 589840 | tf_op jit(solution)/shard_map/reduce_scatter | solution.py:244
  992.3 2.2 convert_element_type.202
  (191 shorter events, 24.8 us)
Async XLA Ops:
  7.2 49.2 %all-gather.12.cloned.1.call-start = ((), (), s32[]{:S(2)}) async-start(), calls=%async_computation.10 | async-start | bytes 1572864 | tf_op jit(solution)/shard_map/all_gather | solution.py:102
  31.2 25.2 %copy-start.23 = (f32[1,1024]{1,0:T(1,128)}, f32[1,1024]{1,0:T(1,128)S(1)}, u32[]{:S(2)}) copy-start(f32[1,1024]{1,0:T(1,128)S(1)} %get-tuple-element.40) | copy-start | bytes 12292
  32.4 4.2 copy-start.29
  34.5 58.7 %all-gather.16.cloned.1.call-start = ((), (), s32[]{:S(2)}) async-start(), calls=%async_computation.12 | async-start | bytes 1114112 | tf_op jit(solution)/shard_map/all_gather | solution.py:125
  35.2 97.1 %all-gather.14.cloned.1.call-start = ((), (), s32[]{:S(2)}) async-start(), calls=%async_computation.11 | async-start | bytes 1114112 | tf_op jit(solution)/shard_map/all_gather | solution.py:126
  36.0 135.3 %all-gather.18.cloned.1.call-start = ((), (), s32[]{:S(2)}) async-start(), calls=%async_computation.13 | async-start | bytes 1114112 | tf_op jit(solution)/shard_map/all_gather | solution.py:127
  36.6 169.1 %reduce-scatter.14.cloned.1.call-start = ((), (), s32[]{:S(2)}) async-start(), calls=%async_computation.14 | async-start | bytes 3145728 | tf_op jit(solution)/shard_map/reduce_scatter | solution.py:106
  54.4 81.0 %copy-start.32 = (f32[64]{0:T(128)}, f32[64]{0:T(128)S(1)}, u32[]{:S(2)}) copy-start(f32[64]{0:T(128)S(1)} %get-tuple-element.41) | copy-start | bytes 772
  54.4 81.4 %copy-start.34 = (f32[64]{0:T(128)}, f32[64]{0:T(128)S(1)}, u32[]{:S(2)}) copy-start(f32[64]{0:T(128)S(1)} %get-tuple-element.42) | copy-start | bytes 772
  55.4 80.4 %copy-start.7 = (f32[512,64]{0,1:T(8,128)}, f32[512,64]{0,1:T(8,128)S(1)}, u32[]{:S(2)}) copy-start(f32[512,64]{0,1:T(8,128)S(1)} %get-tuple-element.38) | copy-start | bytes 393220
  56.4 75.9 %copy-start.2 = (bf16[512,1024]{1,0:T(8,128)(2,1)S(1)}, bf16[512,1024]{1,0:T(8,128)(2,1)}, u32[]{:S(2)}) copy-start(bf16[512,1024]{1,0:T(8,128)(2,1)} %all-gather.12.cloned.1.call-done) | copy-start | bytes 3145732
  133.9 3.0 copy-start.18
  135.4 1.6 copy-start.26
  136.9 2.9 copy-start.10
  138.4 1.5 copy-start.5
  138.4 1.5 copy-start.12
  139.9 3.3 copy-start
  139.9 3.4 copy-start.21
  140.4 2.9 copy-start.16
  141.9 1.5 copy-start.25
  145.6 29.0 %copy-start.17 = (bf16[4,64,2,512]{3,1,2,0:T(8,128)(2,1)}, bf16[4,64,2,512]{3,1,2,0:T(8,128)(2,1)S(1)}, u32[]{:S(2)}) copy-start(bf16[4,64,2,512]{3,1,2,0:T(8,128)(2,1)S(1)} %fusion.21) | copy-start | bytes 1572868
  145.6 60.0 %copy-start.1 = (bf16[256,1024]{1,0:T(8,128)(2,1)S(1)}, bf16[256,1024]{1,0:T(8,128)(2,1)}, u32[]{:S(2)}) copy-start(bf16[256,1024]{1,0:T(8,128)(2,1)} %param.11) | copy-start | bytes 1572868
  174.6 56.1 %all-gather.20.cloned.1.call-start = ((), (), s32[]{:S(2)}) async-start(), calls=%async_computation.15 | async-start | bytes 1572864 | tf_op jit(solution)/shard_map/all_gather | solution.py:102
  209.3 104.7 %all-gather.22.cloned.1.call-start = ((), (), s32[]{:S(2)}) async-start(), calls=%async_computation.16 | async-start | bytes 10027008 | tf_op jit(solution)/shard_map/all_gather | solution.py:157
  210.0 125.2 %all-gather.26.cloned.1.call-start = ((), (), s32[]{:S(2)}) async-start(), calls=%async_computation.19 | async-start | bytes 1572864 | tf_op jit(solution)/shard_map/all_gather | solution.py:102
  210.8 179.9 %all-gather.24.cloned.1.call-start = ((), (), s32[]{:S(2)}) async-start(), calls=%async_computation.17 | async-start | bytes 5013504 | tf_op jit(solution)/shard_map/all_gather | solution.py:158
  211.5 233.2 %reduce-scatter.18.cloned.1.call-start = ((), (), s32[]{:S(2)}) async-start(), calls=%async_computation.20 | async-start | bytes 3145728 | tf_op jit(solution)/shard_map/reduce_scatter | solution.py:106
  314.0 7.6 copy-start.41
  314.0 7.6 copy-start.42
  401.4 6.2 copy-start.46
  401.4 6.2 copy-start.48
  414.1 57.3 %all-gather.28.cloned.1.call-start = ((), (), s32[]{:S(2)}) async-start(), calls=%async_computation.21 | async-start | bytes 1572864 | tf_op jit(solution)/shard_map/all_gather | solution.py:102
  449.9 75.3 %reduce-scatter.20.cloned.1.call-start = ((), (), s32[]{:S(2)}) async-start(), calls=%async_computation.22 | async-start | bytes 3145728 | tf_op jit(solution)/shard_map/reduce_scatter | solution.py:106
  473.7 5.1 slice-start
  473.7 6.0 slice-start.1
  473.7 6.0 copy-start.20
  479.7 2.6 copy-start.11
  482.4 1.1 copy-start.8
  484.8 1.9 copy-start.33
  486.4 4.2 copy-start.14
  486.7 1.5 copy-start.39
  487.2 2.2 copy-start.15
  488.1 2.1 copy-start.13
  490.6 1.9 copy-start.3
  492.5 93.8 %reduce-scatter.22.cloned.1.call-start = ((), (), s32[]{:S(2)}) async-start(), calls=%async_computation.23 | async-start | bytes 1114112 | tf_op jit(solution)/shard_map/reduce_scatter | solution.py:229
  494.3 152.7 %reduce-scatter.24.cloned.1.call-start = ((), (), s32[]{:S(2)}) async-start(), calls=%async_computation.24 | async-start | bytes 1114112 | tf_op jit(solution)/shard_map/reduce_scatter | solution.py:232
  496.3 4.9 copy-start.44
  497.4 209.8 %reduce-scatter.26.cloned.1.call-start = ((), (), s32[]{:S(2)}) async-start(), calls=%async_computation.25 | async-start | bytes 1114112 | tf_op jit(solution)/shard_map/reduce_scatter | solution.py:235
  500.9 284.7 %reduce-scatter.30.cloned.1.call-start = ((), (), s32[]{:S(2)}) async-start(), calls=%async_computation.27 | async-start | bytes 5013504 | tf_op jit(solution)/shard_map/reduce_scatter | solution.py:247
  507.3 7.3 copy-start.43
  507.3 311.5 %reduce-scatter.16.cloned.1.call-start = ((), (), s32[]{:S(2)}) async-start(), calls=%async_computation.18 | async-start | bytes 3145728 | tf_op jit(solution)/shard_map/reduce_scatter | solution.py:106
  514.5 363.4 %reduce-scatter.32.cloned.1.call-start = ((), (), s32[]{:S(2)}) async-start(), calls=%async_computation.28 | async-start | bytes 278528
  514.6 6.1 copy-start.47
  520.8 4.4 copy-start.38
  520.8 4.5 copy-start.40
  520.8 4.5 copy-start.24
  520.8 4.5 copy-start.30
  520.8 6.0 copy-start.31
  532.8 459.5 %reduce-scatter.28.cloned.1.call-start = ((), (), s32[]{:S(2)}) async-start(), calls=%async_computation.26 | async-start | bytes 10027008 | tf_op jit(solution)/shard_map/reduce_scatter | solution.py:244
  541.3 277.6 %copy-start.4 = (f32[256,1024]{1,0:T(8,128)S(1)}, f32[256,1024]{1,0:T(8,128)}, u32[]{:S(2)}) copy-start(f32[256,1024]{1,0:T(8,128)} %reduce-scatter.18.cloned.1.call-done) | copy-start | bytes 3145732
  541.3 277.6 %copy-start.9 = (bf16[256,1024]{1,0:T(8,128)(2,1)S(1)}, bf16[256,1024]{1,0:T(8,128)(2,1)}, u32[]{:S(2)}) copy-start(bf16[256,1024]{1,0:T(8,128)(2,1)} %param.12) | copy-start | bytes 1572868
  541.3 277.6 %copy-start.22 = (f32[1,1024]{1,0:T(1,128)S(1)}, f32[1,1024]{1,0:T(1,128)}, u32[]{:S(2)}) copy-start(f32[1,1024]{1,0:T(1,128)} %get-tuple-element.39) | copy-start | bytes 12292
  541.3 277.6 %copy-start.28 = (f32[256]{0:T(256)S(1)}, f32[256]{0:T(256)}, u32[]{:S(2)}) copy-start(f32[256]{0:T(256)} %copy-done.27) | copy-start | bytes 3076
  541.3 277.6 %copy-start.37 = (f32[256]{0:T(256)S(1)}, f32[256]{0:T(256)}, u32[]{:S(2)}) copy-start(f32[256]{0:T(256)} %copy-done.36) | copy-start | bytes 3076
  (6 other events, 4.5 us)
Sparse Core Ops, SparseCore 0:
  34.6 18.5 all-gather.11
  55.4 37.8 all-gather.15
  95.4 36.8 all-gather.13
  134.3 36.8 all-gather.17
  174.7 30.8 reduce-scatter.13
  209.4 21.2 all-gather.19
  233.0 80.9 all-gather.21
  315.5 19.6 all-gather.25
  337.5 53.0 all-gather.23
  414.2 30.4 reduce-scatter.17
  450.1 21.2 all-gather.27
  492.6 31.8 reduce-scatter.19
  528.7 57.5 reduce-scatter.21
  590.4 56.6 reduce-scatter.23
  650.5 56.6 reduce-scatter.25
  710.9 74.6 reduce-scatter.29
  787.7 31.0 reduce-scatter.15
  822.2 55.7 reduce-scatter.31
  882.1 110.1 reduce-scatter.27
where the time goes:
time: 1010 us; the launch traced here: 1000 us
  waiting for transfers between devices  757 us (75%)
  matrix products  91.5 us (9%)
  blocking collectives  76.2 us (8%)
  other arithmetic  49.7 us (5%)
  between operations  15.9 us (2%)
  local copies, waits for them, and re-layouts  10.2 us (1%)
    reduce_scatter x1, waiting for transfers between devices, on_device(): lax.psum_scatter(grad_gate_up.astype(jnp.bfloat16), 'dp', scatter_dimensi...  113 us
    all_gather x1, waiting for transfers between devices, on_device(): lax.all_gather(w_gate_up, 'dp', axis=1, tiled=True)  83.2 us
    reduce_scatter x1, waiting for transfers between devices, on_device(): lax.psum_scatter(grad_down.astype(jnp.bfloat16), 'dp', scatter_dimension=...  76.9 us
    reduce_scatter x4, waiting for transfers between devices, spread(): return lax.psum_scatter(values, 'tensor', scatter_dimension=0, tiled=True)  62.1 us
    unnamed x20, waiting for transfers between devices  60 us
    reduce_scatter x1, waiting for transfers between devices, on_device(): lax.psum_scatter(grad_kv.astype(jnp.bfloat16), 'dp', scatter_dimension=1,...  59.2 us
    reduce_scatter x1, waiting for transfers between devices, on_device(): lax.psum_scatter(grad_out.astype(jnp.bfloat16), 'dp', scatter_dimension=1...  58.7 us
    all_gather x1, waiting for transfers between devices, on_device(): lax.all_gather(w_down, 'dp', axis=1, tiled=True)  55.4 us
  transfers between devices with their start and end apart: 19, of which 17 were waited for; matrix products, arithmetic and copies ran while one was open for 9% of the time, Pallas kernels for 0%

commit v1 on v0

v1 whole, which is shorter than its diff:
```python
import functools
import math

import jax
import jax.numpy as jnp
from jax import lax
from jax.experimental import pallas as pl
from jax.experimental.pallas import tpu as pltpu
from jax.sharding import PartitionSpec as P

HD = 64


EPSILON = 1e-05
ROPE_BASE = 1000000.0
NEG_FILL = -1e30


def rms_forward(values, gain):
    scale = lax.rsqrt(jnp.mean(values * values, axis=-1, keepdims=True) + EPSILON)
    return (values * scale * gain, scale)


def rms_backward(values, scale, gain, grad):
    weighted = grad * gain
    inner = jnp.mean(weighted * values, axis=-1, keepdims=True)
    return scale * (weighted - values * scale * scale * inner)


def rope_tables(places):
    freqs = ROPE_BASE ** (-jnp.arange(0, HD, 2).astype(jnp.float32) / HD)
    angles = places.astype(jnp.float32)[..., None] * freqs
    angles = jnp.concatenate([angles, angles], axis=-1)
    return (jnp.cos(angles), jnp.sin(angles))


def rotate_half(values):
    half = values.shape[-1] // 2
    return jnp.concatenate([-values[..., half:], values[..., :half]], axis=-1)


def rotate_back(values):
    half = values.shape[-1] // 2
    return jnp.concatenate([values[..., half:], -values[..., :half]], axis=-1)


def allowed_mask(segs):
    length = segs.shape[0]
    index = jnp.arange(length, dtype=jnp.int32)
    return (segs[:, None] == segs[None, :]) & (index[None, :] <= index[:, None])


def contract(left, right, left_dim, right_dim):
    return lax.dot_general(
        left, right, (((left_dim,), (right_dim,)), ((), ())), preferred_element_type=jnp.float32
    )


def fdot(left, right):
    return jnp.dot(left, right, preferred_element_type=jnp.float32)


def row_scores(q_rot, k_rot):
    kv_heads = k_rot.shape[1]
    groups = q_rot.shape[1] // kv_heads
    q_four = q_rot.reshape(q_rot.shape[0], kv_heads, groups, HD)
    scores = jnp.einsum("ikgd,jkd->kgij", q_four, k_rot, preferred_element_type=jnp.float32)
    return (scores / math.sqrt(HD), q_four)


def attend_row(q_rot, k_rot, values, segs):
    scores, q_four = row_scores(q_rot, k_rot)
    allowed = allowed_mask(segs)[None, None]
    masked = jnp.where(allowed, scores, NEG_FILL)
    top = jnp.max(masked, axis=-1, keepdims=True)
    expd = jnp.where(allowed, jnp.exp(masked - top), 0.0)
    total = jnp.sum(expd, axis=-1, keepdims=True)
    probs = (expd / total).astype(jnp.bfloat16)
    log_total = top[..., 0] + jnp.log(total[..., 0])
    attended = jnp.einsum("kgij,jkd->ikgd", probs, values, preferred_element_type=jnp.float32)
    return (attended.reshape(q_rot.shape).astype(jnp.bfloat16), log_total)


def back_row(q_rot, k_rot, values, grad_att, log_total, segs):
    scores, q_four = row_scores(q_rot, k_rot)
    allowed = allowed_mask(segs)[None, None]
    masked = jnp.where(allowed, scores, NEG_FILL)
    probs = jnp.where(allowed, jnp.exp(masked - log_total[..., None]), 0.0)
    probs_b = probs.astype(jnp.bfloat16)
    grad_four = grad_att.reshape(q_four.shape)
    grad_values = jnp.einsum(
        "kgij,ikgd->jkd", probs_b, grad_four, preferred_element_type=jnp.float32
    )
    grad_p = jnp.einsum("ikgd,jkd->kgij", grad_four, values, preferred_element_type=jnp.float32)
    delta = jnp.sum(probs * grad_p, axis=-1, keepdims=True)
    d_scores = (probs * (grad_p - delta) / math.sqrt(HD)).astype(jnp.bfloat16)
    grad_q = jnp.einsum(
        "kgij,jkd->ikgd", d_scores, k_rot, preferred_element_type=jnp.float32
    ).reshape(q_rot.shape)
    grad_k = jnp.einsum("kgij,ikgd->jkd", d_scores, q_four, preferred_element_type=jnp.float32)
    return (grad_q, grad_k, grad_values)


def layout_of(dp):
    if dp == 16:
        return (4, 4, 2)
    return (dp // 4, 2, dp // 2)


class Place:
    def __init__(self, dp):
        self.length, self.zs, self.xs = layout_of(dp)
        me = lax.axis_index("dp")
        self.z = lax.rem(me // self.zs, self.length)
        self.x = lax.rem(me // self.xs, 2)
        self.c = lax.rem(me, 2)

    def device(self, z, x, c):
        return z * self.zs + x * self.xs + c

    def greet(self):
        z, x, c = self.z, self.x, self.c
        barrier = pltpu.get_barrier_semaphore()

        def signal(target):
            pl.semaphore_signal(
                barrier, inc=1, device_id={"dp": target}, device_id_type=pl.DeviceIdType.MESH
            )

        signal(self.device(z, x, 1 - c))
        signal(self.device(z, 1 - x, c))
        pl.when(z > 0)(lambda: signal(self.device(z - 1, x, c)))
        pl.when(z < self.length - 1)(lambda: signal(self.device(z + 1, x, c)))
        ends = jnp.where(z > 0, 1, 0) + jnp.where(z < self.length - 1, 1, 0)
        pl.semaphore_wait(barrier, 2 + ends)


def remote(src, dst, send, recv, target):
    return pltpu.make_async_remote_copy(
        src_ref=src,
        dst_ref=dst,
        send_sem=send,
        recv_sem=recv,
        device_id={"dp": target},
        device_id_type=pl.DeviceIdType.MESH,
    )


def gather_kernel(dp, count, rows, *refs):
    ins, outs = refs[:count], refs[count : 2 * count]
    send, recv, local = refs[2 * count :]
    at = Place(dp)
    z, x, c, length = at.z, at.x, at.c, at.length
    below, above = at.device(z - 1, x, c), at.device(z + 1, x, c)
    beside, sibling = at.device(z, 1 - x, c), at.device(z, x, 1 - c)
    at.greet()
    own = at.device(z, x, c)

    def slab(k, o):
        return outs[k].at[pl.ds(pl.multiple_of(o * rows, rows), rows)]

    for k in range(count):
        pltpu.make_async_copy(ins[k], slab(k, own), local.at[k]).start()

    def move(k, oz, ox, way, target, first):
        o = at.device(oz, ox, c)
        src = ins[k] if first else slab(k, o)
        return remote(src, slab(k, o), send.at[k, oz * 2 + ox, way], recv.at[k, o], target)

    def arrived(k, o):
        remote(slab(k, o), slab(k, o), send.at[k, 0, 0], recv.at[k, o], sibling).wait_recv()

    def steps(act):
        for s in range(length):
            for sign in (1, -1) if s else (0,):
                oz = z - s * sign

                def event(oz=oz, s=s, sign=sign):
                    for k in range(count):
                        act(k, oz, s, sign)

                if s:
                    pl.when((oz >= 0) & (oz < length))(event)
                else:
                    event()
            if s:
                side(s - 1, act)
        side(length - 1, act)

    def side(s, act):
        for sign in (1, -1) if s else (0,):
            oz = z - s * sign

            def event(oz=oz):
                for k in range(count):
                    act(k, oz, None, 0)

            if s:
                pl.when((oz >= 0) & (oz < length))(event)
            else:
                event()

    def begin(k, oz, s, sign):
        if s is None:
            arrived(k, at.device(oz, 1 - x, c))
            move(k, oz, 1 - x, 3, sibling, False).start()
            return
        first = s == 0
        if not first:
            arrived(k, at.device(oz, x, c))
        if sign >= 0:
            pl.when(z < length - 1)(lambda: move(k, oz, x, 0, above, first).start())
        if sign <= 0:
            pl.when(z > 0)(lambda: move(k, oz, x, 1, below, first).start())
        move(k, oz, x, 2, beside, first).start()
        move(k, oz, x, 3, sibling, first).start()

    def finish(k, oz, s, sign):
        if s is None:
            move(k, oz, 1 - x, 3, sibling, False).wait_send()
            return
        first = s == 0
        if sign >= 0:
            pl.when(z < length - 1)(lambda: move(k, oz, x, 0, above, first).wait_send())
        if sign <= 0:
            pl.when(z > 0)(lambda: move(k, oz, x, 1, below, first).wait_send())
        move(k, oz, x, 2, beside, first).wait_send()
        move(k, oz, x, 3, sibling, first).wait_send()

    steps(begin)
    for oz in range(length):
        for ox in range(2):
            for k in range(count):
                arrived(k, at.device(oz, ox, 1 - c))
    steps(finish)
    for k in range(count):
        pltpu.make_async_copy(ins[k], slab(k, own), local.at[k]).wait()


def gather_rows(arrays, dp):
    count, rows = len(arrays), arrays[0].shape[0]
    return pl.pallas_call(
        functools.partial(gather_kernel, dp, count, rows),
        out_shape=[jax.ShapeDtypeStruct((dp * rows, a.shape[1]), a.dtype) for a in arrays],
        in_specs=[pl.BlockSpec(memory_space=pltpu.VMEM)] * count,
        out_specs=[pl.BlockSpec(memory_space=pl.ANY)] * count,
        scratch_shapes=[
            pltpu.SemaphoreType.DMA((count, dp // 2, 4)),
            pltpu.SemaphoreType.DMA((count, dp)),
            pltpu.SemaphoreType.DMA((count,)),
        ],
        compiler_params=pltpu.CompilerParams(collective_id=1, has_side_effects=True),
        name="gather_rows",
    )(*arrays)


def scatter_kernel(dp, count, rows, *refs):
    parts, outs = refs[:count], refs[count : 2 * count]
    mine, first, second, upward, downward = (
        refs[(2 + i) * count : (3 + i) * count] for i in range(5)
    )
    sent1, sent2, sent4, got1, got2, got_up, got_down, local = refs[7 * count :]
    at = Place(dp)
    z, x, c, length = at.z, at.x, at.c, at.length
    below, above = at.device(z - 1, x, c), at.device(z + 1, x, c)
    beside, sibling = at.device(z, 1 - x, c), at.device(z, x, 1 - c)
    at.greet()

    def slab(k, o):
        return parts[k].at[pl.ds(pl.multiple_of(o * rows, rows), rows)]

    def swap(k, t, ox):
        q = t * 2 + ox
        return remote(
            slab(k, at.device(t, ox, 1 - c)), first[k].at[q], sent1.at[k, q], got1.at[k, q], sibling
        )

    def keep(k, t, ox):
        q = t * 2 + ox
        return pltpu.make_async_copy(slab(k, at.device(t, ox, c)), mine[k].at[q], local.at[k, q])

    def cross(k, t):
        q = t * 2 + 1 - x
        return remote(first[k].at[q], second[k].at[t], sent2.at[k, t], got2.at[k, t], beside)

    def rise(k, t):
        return remote(second[k].at[t], upward[k].at[t], sent4.at[k, t], got_up.at[k, t], above)

    def fall(k, t):
        return remote(second[k].at[t], downward[k].at[t], sent4.at[k, t], got_down.at[k, t], below)

    def targets(act):
        for d in range(length - 1, -1, -1):
            for sign in (1, -1) if d else (0,):
                t = z + d * sign

                def event(t=t, sign=sign):
                    for k in range(count):
                        act(k, t, sign)

                if d:
                    pl.when((t >= 0) & (t < length))(event)
                else:
                    event()

    def wide(value):
        return value.astype(jnp.float32)

    def start(k, t, sign):
        for ox in (1 - x, x):
            swap(k, t, ox).start()
            keep(k, t, ox).start()

    def chip_sum(k, t, sign):
        for ox in (1 - x, x):
            q = t * 2 + ox
            keep(k, t, ox).wait()
            swap(k, t, ox).wait_recv()
            first[k][q] = (wide(first[k][q]) + wide(mine[k][q])).astype(jnp.bfloat16)
            if ox is not x:
                cross(k, t).start()

    def chain(k, t, sign):
        cross(k, t).wait_recv()
        if sign == 0:
            outs[k][...] = wide(second[k][t]) + wide(first[k][t * 2 + x])

            def add_up():
                rise(k, t).wait_recv()
                outs[k][...] += wide(upward[k][t])

            def add_down():
                fall(k, t).wait_recv()
                outs[k][...] += wide(downward[k][t])

            pl.when(z > 0)(add_up)
            pl.when(z < length - 1)(add_down)
            return
        base, move = (upward, rise) if sign > 0 else (downward, fall)
        inner = z > 0 if sign > 0 else z < length - 1

        def middle():
            move(k, t).wait_recv()
            second[k][t] = (
                wide(second[k][t]) + wide(first[k][t * 2 + x]) + wide(base[k][t])
            ).astype(jnp.bfloat16)

        def edge():
            second[k][t] = (wide(second[k][t]) + wide(first[k][t * 2 + x])).astype(jnp.bfloat16)

        pl.when(inner)(middle)
        pl.when(jnp.logical_not(inner))(edge)
        move(k, t).start()

    def finish(k, t, sign):
        swap(k, t, 0).wait_send()
        swap(k, t, 1).wait_send()
        cross(k, t).wait_send()
        if sign:
            (rise if sign > 0 else fall)(k, t).wait_send()

    targets(start)
    targets(chip_sum)
    targets(chain)
    targets(finish)


def scatter_rows(arrays, dp):
    count, rows = len(arrays), arrays[0].shape[0] // dp
    length = layout_of(dp)[0]
    slots = [dp // 2, dp // 2, length, length, length]
    return pl.pallas_call(
        functools.partial(scatter_kernel, dp, count, rows),
        out_shape=[jax.ShapeDtypeStruct((rows, a.shape[1]), jnp.float32) for a in arrays],
        in_specs=[pl.BlockSpec(memory_space=pl.ANY)] * count,
        out_specs=[pl.BlockSpec(memory_space=pltpu.VMEM)] * count,
        scratch_shapes=[
            pltpu.VMEM((n, rows, a.shape[1]), a.dtype) for n in slots for a in arrays
        ]
        + [
            pltpu.SemaphoreType.DMA((count, n))
            for n in (dp // 2, length, length, dp // 2, length, length, length, dp // 2)
        ],
        compiler_params=pltpu.CompilerParams(
            collective_id=2, has_side_effects=True, vmem_limit_bytes=60 * 1024 * 1024
        ),
        name="scatter_rows",
    )(*arrays)


def exchange(values):
    return lax.ppermute(values, "tensor", ((0, 1), (1, 0)))


def collect(values):
    if lax.axis_size("tensor") != 2:
        return lax.all_gather(values, "tensor", axis=0, tiled=True)
    other = exchange(values)
    low = lax.axis_index("tensor") == 0
    return jnp.concatenate([jnp.where(low, values, other), jnp.where(low, other, values)])


def spread(values):
    if lax.axis_size("tensor") != 2:
        return lax.psum_scatter(values, "tensor", scatter_dimension=0, tiled=True)
    half = values.shape[0] // 2
    low = lax.axis_index("tensor") == 0
    head, tail = values[:half], values[half:]
    other = exchange(jnp.where(low, tail, head).astype(jnp.bfloat16))
    return jnp.where(low, head, tail) + other.astype(jnp.float32)


def total(values):
    if lax.axis_size("tensor") != 2:
        return lax.psum(values, "tensor")
    return values + exchange(values)


def on_device(
    block_input,
    cotangent,
    segment_ids,
    positions,
    norm_gains,
    qk_gains,
    w_query,
    w_keyval,
    w_output,
    w_gate_up,
    w_down,
):
    dp = lax.axis_size("dp")
    rows_here, row_len = segment_ids.shape
    tokens_here = rows_here * row_len
    shard, q_wide = w_query.shape
    kv_wide, ff_wide = w_keyval.shape[2], w_gate_up.shape[2]
    qk_shard = qk_gains.shape[1]
    gains = jnp.concatenate(
        [norm_gains.T, jnp.pad(qk_gains.T, ((0, shard - qk_shard), (0, 0)))], axis=1
    )
    gains = jnp.pad(gains, ((0, 0), (0, 124)))
    attn_pack = jnp.concatenate([w_query, w_keyval[0], w_keyval[1], w_output.T, gains], axis=1)
    gate_up_pack = jnp.concatenate([w_gate_up[0], w_gate_up[1]], axis=1)
    attn_full, gate_up_full, down_full = gather_rows([attn_pack, gate_up_pack, w_down.T], dp)
    qkv_wide = q_wide + 2 * kv_wide
    qkv_full = attn_full[:, :qkv_wide]
    output_full = attn_full[:, qkv_wide : qkv_wide + q_wide]
    gain_cols = attn_full[:, qkv_wide + q_wide :].astype(jnp.float32)
    gain_attn, gain_ffn = gain_cols[:, 0], gain_cols[:, 1]
    qk_cols = gain_cols.reshape(dp, shard, 128)[:, :qk_shard, 2:4].reshape(dp * qk_shard, 2)
    gain_q, gain_k = qk_cols[:, 0], qk_cols[:, 1]
    heads_here = q_wide // HD
    kv_here = kv_wide // HD
    dy_rows = collect(cotangent)
    xlocal = block_input.astype(jnp.float32)
    normed_f, scale1 = rms_forward(xlocal, gain_attn)
    normed1 = collect(normed_f.astype(jnp.bfloat16))
    qkv = fdot(normed1, qkv_full)
    query = qkv[:, :q_wide].reshape(rows_here, row_len, heads_here, HD)
    keys = qkv[:, q_wide : q_wide + kv_wide].reshape(rows_here, row_len, kv_here, HD)
    values = (
        qkv[:, q_wide + kv_wide :].astype(jnp.bfloat16).reshape(rows_here, row_len, kv_here, HD)
    )
    q_norm, q_scale = rms_forward(query, gain_q)
    k_norm, k_scale = rms_forward(keys, gain_k)
    cosv, sinv = rope_tables(positions)
    cosv = cosv[:, :, None, :]
    sinv = sinv[:, :, None, :]
    q_rot = (q_norm * cosv + rotate_half(q_norm) * sinv).astype(jnp.bfloat16)
    k_rot = (k_norm * cosv + rotate_half(k_norm) * sinv).astype(jnp.bfloat16)
    attended, log_total = jax.vmap(attend_row)(q_rot, k_rot, values, segment_ids)
    att_flat = attended.reshape(tokens_here, heads_here * HD)
    hidden = xlocal + spread(contract(att_flat, output_full, 1, 1))
    normed_g, scale2 = rms_forward(hidden, gain_ffn)
    normed2 = collect(normed_g.astype(jnp.bfloat16))
    gate_up = fdot(normed2, gate_up_full)
    gate_proj, up_proj = gate_up[:, :ff_wide], gate_up[:, ff_wide:]
    sigmoid_gate = jax.nn.sigmoid(gate_proj)
    silu_gate = gate_proj * sigmoid_gate
    act = (silu_gate * up_proj).astype(jnp.bfloat16)
    block_output = (hidden + spread(contract(act, down_full, 1, 1))).astype(jnp.bfloat16)
    grad_act = fdot(dy_rows, down_full)
    grad_down = contract(dy_rows, act, 0, 0).astype(jnp.bfloat16)
    d_gate = grad_act * up_proj * sigmoid_gate * (1.0 + gate_proj * (1.0 - sigmoid_gate))
    d_gate_up = jnp.concatenate(
        [d_gate.astype(jnp.bfloat16), (grad_act * silu_gate).astype(jnp.bfloat16)], axis=1
    )
    grad_gate_up = contract(normed2, d_gate_up, 0, 0).astype(jnp.bfloat16)
    grad_n2 = spread(contract(d_gate_up, gate_up_full, 1, 1))
    gain_ffn_grad = jnp.sum(grad_n2 * hidden * scale2, axis=0)
    grad_hidden = cotangent.astype(jnp.float32) + rms_backward(hidden, scale2, gain_ffn, grad_n2)
    grad_rows = collect(grad_hidden.astype(jnp.bfloat16))
    grad_att = (
        fdot(grad_rows, output_full)
        .astype(jnp.bfloat16)
        .reshape(rows_here, row_len, heads_here, HD)
    )
    grad_out = contract(grad_rows, att_flat, 0, 0).astype(jnp.bfloat16)
    grad_qrot, grad_krot, grad_vals = jax.vmap(back_row)(
        q_rot, k_rot, values, grad_att, log_total, segment_ids
    )
    grad_qn = grad_qrot * cosv + rotate_back(grad_qrot * sinv)
    grad_kn = grad_krot * cosv + rotate_back(grad_krot * sinv)
    gain_q_grad = jnp.sum(grad_qn * query * q_scale, axis=(0, 1, 2))
    gain_k_grad = jnp.sum(grad_kn * keys * k_scale, axis=(0, 1, 2))
    d_query = rms_backward(query, q_scale, gain_q, grad_qn).astype(jnp.bfloat16)
    d_keys = rms_backward(keys, k_scale, gain_k, grad_kn).astype(jnp.bfloat16)
    d_qkv = jnp.concatenate(
        [
            d_query.reshape(tokens_here, q_wide),
            d_keys.reshape(tokens_here, kv_wide),
            grad_vals.astype(jnp.bfloat16).reshape(tokens_here, kv_wide),
        ],
        axis=1,
    )
    grad_qkv = contract(normed1, d_qkv, 0, 0).astype(jnp.bfloat16)
    grad_n1 = spread(contract(d_qkv, qkv_full, 1, 1))
    gain_attn_grad = jnp.sum(grad_n1 * xlocal * scale1, axis=0)
    grad_input = grad_hidden + rms_backward(xlocal, scale1, gain_attn, grad_n1)
    gain_terms = total(
        jnp.concatenate([gain_attn_grad, gain_ffn_grad, gain_q_grad, gain_k_grad])[None]
    )[0]
    wide = dp * shard
    norm_terms = gain_terms[: 2 * wide].reshape(2, wide).T
    qk_terms = gain_terms[2 * wide :].reshape(2, dp, qk_shard).transpose(1, 2, 0)
    qk_terms = jnp.pad(qk_terms, ((0, 0), (0, shard - qk_shard), (0, 0))).reshape(wide, 2)
    gain_pack = jnp.concatenate([norm_terms, qk_terms], axis=1).astype(jnp.bfloat16)
    gain_pack = jnp.pad(gain_pack, ((0, 0), (0, 124)))
    grad_attn = jnp.concatenate([grad_qkv, grad_out, gain_pack], axis=1)
    attn_sum, gate_up_sum, down_sum = scatter_rows([grad_attn, grad_gate_up, grad_down], dp)
    gain_sum = attn_sum[:, qkv_wide + q_wide :]
    return (
        block_output,
        grad_input,
        gain_sum[:, 0:2].T,
        gain_sum[:qk_shard, 2:4].T,
        attn_sum[:, :q_wide],
        jnp.stack([attn_sum[:, q_wide : q_wide + kv_wide], attn_sum[:, q_wide + kv_wide : qkv_wide]]),
        attn_sum[:, qkv_wide : qkv_wide + q_wide].T,
        jnp.stack([gate_up_sum[:, :ff_wide], gate_up_sum[:, ff_wide:]]),
        down_sum.T,
    )


def solution(mesh):
    return jax.shard_map(
        on_device,
        mesh=mesh,
        in_specs=(
            P(("dp", "tensor"), None),
            P(("dp", "tensor"), None),
            P("dp", None),
            P("dp", None),
            P(None, "dp"),
            P(None, "dp"),
            P("dp", "tensor"),
            P(None, "dp", "tensor"),
            P("tensor", "dp"),
            P(None, "dp", "tensor"),
            P("tensor", "dp"),
        ),
        out_specs=(
            P(("dp", "tensor"), None),
            P(("dp", "tensor"), None),
            P(None, "dp"),
            P(None, "dp"),
            P("dp", "tensor"),
            P(None, "dp", "tensor"),
            P("tensor", "dp"),
            P(None, "dp", "tensor"),
            P("tensor", "dp"),
        ),
        check_vma=False,
    )
```

time: 1010 us -> 428 us (0.42)
  waiting for transfers between devices: 757 us -> 43.3 us
  Pallas kernels: 0 us -> 205 us
  blocking collectives: 76.2 us -> 0 us
  local copies, waits for them, and re-layouts: 10.2 us -> 41.6 us
  matrix products: 91.5 us -> 73.8 us
  between operations: 15.9 us -> 2.07 us
  starting transfers between devices: 1.4 us -> 12 us
    reduce_scatter x9 -> x0, waiting for transfers between devices: 413 us -> none  [the longest x1 113 us: on_device(): lax.psum_scatter(grad_gate_up.astype(jnp.bfloat16), 'dp', scatter_dimensi...]
    all_gather x9 -> x0, waiting for transfers between devices: 283 us -> none  [the longest x1 83.2 us: on_device(): lax.all_gather(w_gate_up, 'dp', axis=1, tiled=True)]
    pallas_call x0 -> x2, Pallas kernels: none -> 205 us  [the longest x1 103 us: gather_rows(): pl.pallas_call(functools.partial(gather_kernel, dp, count, rows), out_sha...]
    unnamed x20 -> x0, waiting for transfers between devices: 60 us -> none
    ppermute x0 -> x9, waiting for transfers between devices: none -> 43.3 us  [exchange(): return lax.ppermute(values, 'tensor', ((0, 1), (1, 0)))]
    all_gather x2 -> x0, blocking collectives: 40.9 us -> none  [the longest x1 23.3 us: on_device(): lax.all_gather(norm_gains, 'dp', axis=1, tiled=True)]
    unnamed x1 -> x0, blocking collectives: 30.2 us -> none
    dot_general x14 -> x8, matrix products: 52.3 us -> 34.3 us  [contract(): lax.dot_general(left, right, (((left_dim,), (right_dim,)), ((), ())), pre...]
  transfers between devices with their start and end apart: 19 -> 9, of which waited for: 17 -> 7; matrix products, arithmetic and copies ran while one was open for 9% -> 11% of each run, Pallas kernels for 0% -> 0%
where the time goes in v1:
time: 428 us; the launch traced here: 420 us
  Pallas kernels  205 us (48%)
  matrix products  73.8 us (17%)
  waiting for transfers between devices  43.3 us (10%)
  other arithmetic  42.3 us (10%)
  local copies, waits for them, and re-layouts  41.6 us (10%)
  starting transfers between devices  12 us (3%)
    pallas_call x1, Pallas kernels, gather_rows(): pl.pallas_call(functools.partial(gather_kernel, dp, count, rows), out_sha...  103 us
    pallas_call x1, Pallas kernels, scatter_rows(): pl.pallas_call(functools.partial(scatter_kernel, dp, count, rows), out_sh...  101 us
    ppermute x9, waiting for transfers between devices, exchange(): return lax.ppermute(values, 'tensor', ((0, 1), (1, 0)))  43.3 us
    dot_general x8, matrix products, contract(): lax.dot_general(left, right, (((left_dim,), (right_dim,)), ((), ())), pre...  34.3 us
    dot_general x4, matrix products, fdot(): return jnp.dot(left, right, preferred_element_type=jnp.float32)  26.2 us
    ppermute x9, starting transfers between devices, exchange(): return lax.ppermute(values, 'tensor', ((0, 1), (1, 0)))  12 us
  transfers between devices with their start and end apart: 9, of which 7 were waited for; matrix products, arithmetic and copies ran while one was open for 11% of the time, Pallas kernels for 0%

profile of v1, /device:TPU:0, one launch (start us, length us, event | category | flops | bytes accessed | tf_op | source)
XLA Modules:
  0.0 419.7 jit_solution(13718324065677092545)
XLA Ops:
  0.7 1.3 fusion.41
  5.1 1.1 slice_bitcast_fusion.3
  8.0 103.2 %gather_rows.1 = (bf16[1024,1664]{1,0:T(8,128)(2,1)}, bf16[1024,4608]{1,0:T(8,128)(2,1)}, bf16[1024,2304]{1,0:T(8,128)(2,1)}) custom-call(bf16[64,1664]{1,0:T(8,128)(2,1)} %copy-done.31, bf16[64,4608]{1,0:T(8,128)(2,1)} %pad_maximum_fusion.18.refs_1_, bf16[64,2304]{1,0:T(8,128)(2,1)} %bitcast.185), custom_call_target="tpu_custom_call" | custom-call | tf_op jit(solution)/shard_map/gather_rows/pallas_call | solution.py:242
  113.4 1.6 collective-permute-start
  116.4 11.4 %collective-permute-done = bf16[256,1024]{1,0:T(8,128)(2,1)S(1)} collective-permute-done((bf16[256,1024]{1,0:T(8,128)(2,1)S(1)}, bf16[256,1024]{1,0:T(8,128)(2,1)S(1)}, u32[]{:S(2)}, u32[]{:S(2)}) %collective-permute-start) | collective-permute-done | bytes 524320 | tf_op jit(solution)/shard_map/ppermute | solution.py:392
  128.1 3.2 fusion.19
  134.3 1.2 copy.106
  136.6 1.6 copy.109
  139.5 1.5 fusion.81
  141.1 1.5 fusion.4
  142.6 1.8 copy-done
  144.5 2.7 fusion.21
  147.2 2.2 fusion.53
  149.5 1.6 collective-permute-start.1
  151.6 12.8 %collective-permute-done.1 = bf16[256,1024]{1,0:T(8,128)(2,1)S(1)} collective-permute-done((bf16[256,1024]{1,0:T(8,128)(2,1)S(1)}, bf16[256,1024]{1,0:T(8,128)(2,1)S(1)}, u32[]{:S(2)}, u32[]{:S(2)}) %collective-permute-start.1) | collective-permute-done | bytes 524320 | tf_op jit(solution)/shard_map/ppermute | solution.py:392
  165.7 1.5 collective-permute-start.2
  167.2 1.1 mul.635
  168.3 2.5 copy.114
  170.8 1.2 mul.640
  172.0 1.3 mul.641
  173.3 1.1 mul.631
  174.4 2.5 copy.119
  177.7 1.3 broadcast_select_fusion.3
  179.0 6.6 %collective-permute-done.2 = bf16[256,1024]{1,0:T(8,128)(2,1)} collective-permute-done((bf16[256,1024]{1,0:T(8,128)(2,1)}, bf16[256,1024]{1,0:T(8,128)(2,1)}, u32[]{:S(2)}, u32[]{:S(2)}) %collective-permute-start.2) | collective-permute-done | bytes 524320 | tf_op jit(solution)/shard_map/ppermute | solution.py:392
  185.6 1.5 broadcast_select_fusion.5
  187.1 11.7 %fusion.56 = f32[512,4608]{1,0:T(8,128)} fusion(bf16[1024,4608]{1,0:T(8,128)(2,1)} %get-tuple-element.16, bf16[256,1024]{1,0:T(8,128)(2,1)S(1)} %get-tuple-element.88, bf16[256,1024]{1,0:T(8,128)(2,1)S(1)} %get-tuple-element.87), kind=kOutput, calls=%fused_computation.100 | convolution fusion | flops 4833935360 | bytes 19922944 | tf_op jit(solution)/shard_map/dot_general | solution.py:60
  198.8 8.9 %multiply_convert_fusion.1 = (bf16[512,2304]{1,0:T(8,128)(2,1)}, bf16[512,2304]{1,0:T(8,128)(2,1)}, bf16[512,2304]{1,0:T(8,128)(2,1)}) fusion(f32[512,4608]{1,0:T(8,128)} %fusion.56, bf16[1024,2304]{1,0:T(8,128)(2,1)S(1)} %bitcast.209, bf16[256,1024]{1,0:T(8,128)(2,1)S(1)} %get-tuple-element.86, bf16[256,1024]{1,0:T(8,128)(2,1)S(1)} %get-tuple-element.85), kind=kOutput, calls=%fused_computation.18 | convolution fusion | flops 2435710976 | bytes 22282240 | tf_op jit(solution)/shard_map/dot_general | solution.py:60
  207.7 6.9 %fusion.16 = f32[512,1024]{1,0:T(8,128)S(1)} fusion(bf16[1024,4608]{1,0:T(8,128)(2,1)S(1)} %bitcast.207, bf16[512,2304]{1,0:T(8,128)(2,1)} %get-tuple-element.71, bf16[512,2304]{1,0:T(8,128)(2,1)} %get-tuple-element.70), kind=kOutput, calls=%fused_computation.29 | convolution fusion | flops 4841275392 | bytes 16252928 | tf_op jit(solution)/shard_map/dot_general | solution.py:54
  214.8 1.6 collective-permute-start.5
  216.4 10.0 %convolution_convert_fusion.refs_1_ = bf16[1024,4608]{1,0:T(8,128)(2,1)} fusion(bf16[512,2304]{1,0:T(8,128)(2,1)} %get-tuple-element.71, bf16[512,2304]{1,0:T(8,128)(2,1)} %get-tuple-element.70, bf16[256,1024]{1,0:T(8,128)(2,1)S(1)} %get-tuple-element.88, bf16[256,1024]{1,0:T(8,128)(2,1)S(1)} %get-tuple-element.87), kind=kOutput, calls=%fused_computation | convolution fusion | flops 4848091136 | bytes 15204352 | tf_op jit(solution)/shard_map/dot_general | solution.py:54
  228.0 1.8 fusion.77
  229.8 1.6 collective-permute-start.6
  231.3 4.0 fusion.82
  235.3 4.3 %convolution_convert_fusion.1.refs_2_ = bf16[1024,2304]{1,0:T(8,128)(2,1)} fusion(bf16[512,2304]{1,0:T(8,128)(2,1)S(1)} %copy-done.55, bf16[256,1024]{1,0:T(8,128)(2,1)S(1)} %get-tuple-element.86, bf16[256,1024]{1,0:T(8,128)(2,1)S(1)} %get-tuple-element.85), kind=kOutput, calls=%fused_computation.14 | convolution fusion | flops 2420375552 | bytes 8126464 | tf_op jit(solution)/shard_map/dot_general | solution.py:54
  239.7 1.9 collective-permute-done.6
  241.6 2.4 convolution_convert_fusion.4
  244.1 2.3 fusion.29
  246.3 2.7 fusion
  249.1 2.8 fusion.9
  251.9 2.3 broadcast_multiply_fusion
  254.3 1.8 fusion.83
  256.1 1.8 copy.123
  259.0 1.9 multiply_reduce_fusion.5
  261.8 1.1 copy.122
  262.9 1.5 bitcast_multiply_fusion.2
  264.5 1.2 pad_maximum_fusion.8
  265.8 2.5 copy.115
  268.3 2.5 copy.113
  271.0 1.3 copy.118
  272.3 3.8 multiply_reduce_fusion
  276.1 1.3 fusion.17
  278.4 1.5 collective-permute-start.7
  281.5 3.8 convolution_convert_fusion.2
  285.4 1.7 convolution_convert_fusion.3
  287.1 6.4 %collective-permute-done.7 = bf16[256,1024]{1,0:T(8,128)(2,1)} collective-permute-done((bf16[256,1024]{1,0:T(8,128)(2,1)}, bf16[256,1024]{1,0:T(8,128)(2,1)}, u32[]{:S(2)}, u32[]{:S(2)}) %collective-permute-start.7) | collective-permute-done | bytes 524320 | tf_op jit(solution)/shard_map/ppermute | solution.py:392
  293.5 2.4 fusion.44
  296.0 1.6 collective-permute-start.8
  297.6 3.3 collective-permute-done.3
  300.8 3.8 fusion.36
  305.2 3.2 fusion.15.refs_0_
  308.4 101.5 %scatter_rows.1 = (f32[64,1664]{1,0:T(8,128)}, f32[64,4608]{1,0:T(8,128)}, f32[64,2304]{1,0:T(8,128)}) custom-call(bf16[1024,1664]{1,0:T(8,128)(2,1)} %fusion.15.refs_0_, bf16[1024,4608]{1,0:T(8,128)(2,1)} %convolution_convert_fusion.refs_1_, bf16[1024,2304]{1,0:T(8,128)(2,1)} %convolution_convert_fusion.1.refs_2_), custom_call_target="tpu_custom_call" | custom-call | tf_op jit(solution)/shard_map/scatter_rows/pallas_call | solution.py:372
  411.5 1.7 slice_bitcast_fusion.5
  415.3 1.3 slice_bitcast_fusion.1
  417.3 1.1 pad_maximum_fusion.3
  (208 shorter events, 29.0 us)
Async XLA Ops:
  0.6 112.5 %copy-start.1 = (bf16[256,1024]{1,0:T(8,128)(2,1)S(1)}, bf16[256,1024]{1,0:T(8,128)(2,1)}, u32[]{:S(2)}) copy-start(bf16[256,1024]{1,0:T(8,128)(2,1)} %param.11) | copy-start | bytes 1572868
  0.7 114.5 %copy-start.53 = (s32[1,512]{1,0:T(1,128)S(1)}, s32[1,512]{1,0:T(1,128)}, u32[]{:S(2)}) copy-start(s32[1,512]{1,0:T(1,128)} %param.14) | copy-start | bytes 6148
  0.7 115.5 %copy-start.51 = (s32[1,512]{1,0:T(1,128)S(1)}, s32[1,512]{1,0:T(1,128)}, u32[]{:S(2)}) copy-start(s32[1,512]{1,0:T(1,128)} %param.13) | copy-start | bytes 6148
  2.0 126.1 %copy-start.44 = (f32[256]{0:T(256)}, f32[256]{0:T(256)S(1)}, u32[]{:S(2)}) copy-start(f32[256]{0:T(256)S(1)} %add_rsqrt_fusion.3) | copy-start | bytes 3076
  113.2 14.9 %copy-start.39 = (f32[1024]{0:T(1024)}, f32[1024]{0:T(1024)S(1)}, u32[]{:S(2)}) copy-start(f32[1024]{0:T(1024)S(1)} %get-tuple-element.64) | copy-start | bytes 12292
  113.4 14.4 %collective-permute-start = (bf16[256,1024]{1,0:T(8,128)(2,1)S(1)}, bf16[256,1024]{1,0:T(8,128)(2,1)S(1)}, u32[]{:S(2)}, u32[]{:S(2)}) collective-permute-start(bf16[256,1024]{1,0:T(8,128)(2,1)S(1)} %fusion.32), channel_id=1, source_target_pairs={{0,1},{1,0},{2,3},{3,2},{4,5},{5,4},{6,7},{7,6},{8,9},{9,8},{10,11... | collective-permute-start | bytes 1572872 | tf_op jit(solution)/shard_map/ppermute | solution.py:392
  115.2 20.4 %copy-start.48 = (f32[64,1]{0,1:T(1,128)}, f32[64,1]{0,1:T(1,128)S(1)}, u32[]{:S(2)}) copy-start(f32[64,1]{0,1:T(1,128)S(1)} %copy.142) | copy-start | bytes 772
  116.1 23.0 %copy-start.7 = (f32[512,64]{0,1:T(8,128)}, f32[512,64]{0,1:T(8,128)S(1)}, u32[]{:S(2)}) copy-start(f32[512,64]{0,1:T(8,128)S(1)} %get-tuple-element.104) | copy-start | bytes 393220
  128.1 3.3 copy-start.27
  128.1 3.3 copy-start.29
  134.3 4.2 copy-start.46
  135.6 3.2 copy-start.34
  135.7 3.1 copy-start.49
  141.1 3.4 copy-start
  141.1 3.4 copy-start.38
  141.1 3.4 copy-start.16
  142.6 4.6 %copy-start.41 = (f32[4,2,512]{2,1,0:T(2,128)}, f32[4,2,512]{2,1,0:T(2,128)S(1)}, u32[]{:S(2)}) copy-start(f32[4,2,512]{2,1,0:T(2,128)S(1)} %fusion.4) | copy-start | bytes 49156
  147.2 4.4 %copy-start.21 = (bf16[4,64,2,512]{3,1,2,0:T(8,128)(2,1)}, bf16[4,64,2,512]{3,1,2,0:T(8,128)(2,1)S(1)}, u32[]{:S(2)}) copy-start(bf16[4,64,2,512]{3,1,2,0:T(8,128)(2,1)S(1)} %fusion.21) | copy-start | bytes 1572868
  147.2 17.5 %copy-start.36 = (f32[1024]{0:T(1024)S(1)}, f32[1024]{0:T(1024)}, u32[]{:S(2)}) copy-start(f32[1024]{0:T(1024)} %get-tuple-element.63) | copy-start | bytes 12292
  149.5 14.9 %collective-permute-start.1 = (bf16[256,1024]{1,0:T(8,128)(2,1)S(1)}, bf16[256,1024]{1,0:T(8,128)(2,1)S(1)}, u32[]{:S(2)}, u32[]{:S(2)}) collective-permute-start(bf16[256,1024]{1,0:T(8,128)(2,1)S(1)} %select_convert_fusion.3), channel_id=1, source_target_pairs={{0,1},{1,0},{2,3},{3,2},{4,5},{5,4},{6,7},{7,6},{8,9},{9,8},{10,11... | collective-permute-start | bytes 1572872 | tf_op jit(solution)/shard_map/ppermute | solution.py:392
  151.1 26.7 %collective-permute-start.4 = (bf16[256,1024]{1,0:T(8,128)(2,1)}, bf16[256,1024]{1,0:T(8,128)(2,1)}, u32[]{:S(2)}, u32[]{:S(2)}) collective-permute-start(bf16[256,1024]{1,0:T(8,128)(2,1)} %param.12), channel_id=1, source_target_pairs={{0,1},{1,0},{2,3},{3,2},{4,5},{5,4},{6,7},{7,6},{8,9},{9,8},{10,11... | collective-permute-start | bytes 1572872 | tf_op jit(solution)/shard_map/ppermute | solution.py:392
  165.7 19.9 %collective-permute-start.2 = (bf16[256,1024]{1,0:T(8,128)(2,1)}, bf16[256,1024]{1,0:T(8,128)(2,1)}, u32[]{:S(2)}, u32[]{:S(2)}) collective-permute-start(bf16[256,1024]{1,0:T(8,128)(2,1)} %multiply_convert_fusion.3), channel_id=1, source_target_pairs={{0,1},{1,0},{2,3},{3,2},{4,5},{5,4},{6,7},{7,6},{8,9},{9,8},{10,11... | collective-permute-start | bytes 1572872 | tf_op jit(solution)/shard_map/ppermute | solution.py:392
  174.4 11.1 %copy-start.37 = (f32[1024]{0:T(1024)S(1)}, f32[1024]{0:T(1024)}, u32[]{:S(2)}) copy-start(f32[1024]{0:T(1024)} %get-tuple-element.63) | copy-start | bytes 12292
  174.4 11.1 %copy-start.43 = (f32[256]{0:T(256)S(1)}, f32[256]{0:T(256)}, u32[]{:S(2)}) copy-start(f32[256]{0:T(256)} %copy-done.42) | copy-start | bytes 3076
  185.6 13.2 %slice-start.5 = ((s8[4718592]{0:T(1024)(128)(4,1)}), s8[4194304]{0:T(1024)(128)(4,1)S(1)}, s32[]{:S(2)}) async-start(s8[4718592]{0:T(1024)(128)(4,1)} %bitcast.208), calls=%async_computation.5 | async-start | bytes 8388608
  187.1 11.7 %slice-start.6 = ((s8[4718592]{0:T(1024)(128)(4,1)}), s8[524288]{0:T(1024)(128)(4,1)S(1)}, s32[]{:S(2)}) async-start(s8[4718592]{0:T(1024)(128)(4,1)} %bitcast.208), calls=%async_computation.6 | async-start | bytes 1048576
  187.1 20.6 %slice-start.2 = ((s8[9437184]{0:T(1024)(128)(4,1)}), s8[4194304]{0:T(1024)(128)(4,1)S(1)}, s32[]{:S(2)}) async-start(s8[9437184]{0:T(1024)(128)(4,1)} %bitcast.206), calls=%async_computation.2 | async-start | bytes 8388608
  198.8 8.9 %slice-start.3 = ((s8[9437184]{0:T(1024)(128)(4,1)}), s8[4194304]{0:T(1024)(128)(4,1)S(1)}, s32[]{:S(2)}) async-start(s8[9437184]{0:T(1024)(128)(4,1)} %bitcast.206), calls=%async_computation.3 | async-start | bytes 8388608
  198.8 8.9 %slice-start.4 = ((s8[9437184]{0:T(1024)(128)(4,1)}), s8[1048576]{0:T(1024)(128)(4,1)S(1)}, s32[]{:S(2)}) async-start(s8[9437184]{0:T(1024)(128)(4,1)} %bitcast.206), calls=%async_computation.4 | async-start | bytes 2097152
  214.8 12.7 %collective-permute-start.5 = (bf16[256,1024]{1,0:T(8,128)(2,1)S(1)}, bf16[256,1024]{1,0:T(8,128)(2,1)S(1)}, u32[]{:S(2)}, u32[]{:S(2)}) collective-permute-start(bf16[256,1024]{1,0:T(8,128)(2,1)S(1)} %select_convert_fusion.1), channel_id=1, source_target_pairs={{0,1},{1,0},{2,3},{3,2},{4,5},{5,4},{6,7},{7,6},{8,9},{9,8},{10,11... | collective-permute-start | bytes 1572872 | tf_op jit(solution)/shard_map/ppermute | solution.py:392
  226.4 4.9 %copy-start.55 = (bf16[512,2304]{1,0:T(8,128)(2,1)S(1)}, bf16[512,2304]{1,0:T(8,128)(2,1)}, u32[]{:S(2)}) copy-start(bf16[512,2304]{1,0:T(8,128)(2,1)} %get-tuple-element.72) | copy-start | bytes 7077892
  227.9 3.4 copy-start.3
  229.8 11.8 %collective-permute-start.6 = (bf16[256,1024]{1,0:T(8,128)(2,1)S(1)}, bf16[256,1024]{1,0:T(8,128)(2,1)S(1)}, u32[]{:S(2)}, u32[]{:S(2)}) collective-permute-start(bf16[256,1024]{1,0:T(8,128)(2,1)S(1)} %fusion.77), channel_id=1, source_target_pairs={{0,1},{1,0},{2,3},{3,2},{4,5},{5,4},{6,7},{7,6},{8,9},{9,8},{10,11... | collective-permute-start | bytes 1572872 | tf_op jit(solution)/shard_map/ppermute | solution.py:392
  231.3 12.7 %slice-start = ((s8[8388608]{0:T(1024)(128)(4,1)}), s8[4194304]{0:T(1024)(128)(4,1)S(1)}, s32[]{:S(2)}) async-start(s8[8388608]{0:T(1024)(128)(4,1)} %bitcast.160), calls=%async_computation | async-start | bytes 8388608
  235.3 8.7 %slice-start.1 = ((s8[8388608]{0:T(1024)(128)(4,1)}), s8[4194304]{0:T(1024)(128)(4,1)S(1)}, s32[]{:S(2)}) async-start(s8[8388608]{0:T(1024)(128)(4,1)} %bitcast.160), calls=%async_computation.1 | async-start | bytes 8388608
  241.6 4.7 %copy-start.23 = (bf16[256,1024]{1,0:T(8,128)(2,1)}, bf16[256,1024]{1,0:T(8,128)(2,1)S(1)}, u32[]{:S(2)}) copy-start(bf16[256,1024]{1,0:T(8,128)(2,1)S(1)} %get-tuple-element.83) | copy-start | bytes 1572868
  241.6 4.7 %copy-start.25 = (bf16[256,1024]{1,0:T(8,128)(2,1)}, bf16[256,1024]{1,0:T(8,128)(2,1)S(1)}, u32[]{:S(2)}) copy-start(bf16[256,1024]{1,0:T(8,128)(2,1)S(1)} %get-tuple-element.84) | copy-start | bytes 1572868
  244.0 2.3 copy-start.17
  249.0 2.9 copy-start.6
  249.0 2.9 copy-start.8
  251.9 2.4 copy-start.15
  254.3 4.7 %copy-start.35 = (f32[512,4]{0,1:T(4,128)S(1)}, f32[512,4]{0,1:T(4,128)}, u32[]{:S(2)}) copy-start(f32[512,4]{0,1:T(4,128)} %copy-done.34) | copy-start | bytes 24580
  254.3 4.7 %copy-start.50 = (f32[64,1]{0,1:T(1,128)S(1)}, f32[64,1]{0,1:T(1,128)}, u32[]{:S(2)}) copy-start(f32[64,1]{0,1:T(1,128)} %copy-done.48) | copy-start | bytes 772
  256.1 6.8 %copy-start.9 = (f32[512,64]{0,1:T(8,128)S(1)}, f32[512,64]{0,1:T(8,128)}, u32[]{:S(2)}) copy-start(f32[512,64]{0,1:T(8,128)} %copy-done.7) | copy-start | bytes 393220
  259.0 5.4 %copy-start.47 = (f32[64,1]{0,1:T(1,128)S(1)}, f32[64,1]{0,1:T(1,128)}, u32[]{:S(2)}) copy-start(f32[64,1]{0,1:T(1,128)} %copy.143) | copy-start | bytes 772
  262.9 13.2 %copy-start.33 = (bf16[512,256]{1,0:T(8,128)(2,1)}, bf16[512,256]{1,0:T(8,128)(2,1)S(1)}, u32[]{:S(2)}) copy-start(bf16[512,256]{1,0:T(8,128)(2,1)S(1)} %copy.122) | copy-start | bytes 786436
  265.8 6.5 %copy-start.52 = (f32[512]{0:T(512)S(1)}, f32[512]{0:T(512)}, u32[]{:S(2)}) copy-start(f32[512]{0:T(512)} %mul.641) | copy-start | bytes 6148
  271.0 5.1 %copy-start.32 = (bf16[512,256]{1,0:T(8,128)(2,1)S(1)}, bf16[512,256]{1,0:T(8,128)(2,1)}, u32[]{:S(2)}) copy-start(bf16[512,256]{1,0:T(8,128)(2,1)} %copy.123) | copy-start | bytes 786436
  272.3 3.8 copy-start.30
  276.1 3.8 copy-start.10
  276.1 5.3 %copy-start.28 = (bf16[256,1024]{1,0:T(8,128)(2,1)S(1)}, bf16[256,1024]{1,0:T(8,128)(2,1)}, u32[]{:S(2)}) copy-start(bf16[256,1024]{1,0:T(8,128)(2,1)} %copy-done.27) | copy-start | bytes 1572868
  277.4 3.4 copy-start.11
  278.4 15.1 %collective-permute-start.7 = (bf16[256,1024]{1,0:T(8,128)(2,1)}, bf16[256,1024]{1,0:T(8,128)(2,1)}, u32[]{:S(2)}, u32[]{:S(2)}) collective-permute-start(bf16[256,1024]{1,0:T(8,128)(2,1)} %select_convert_fusion), channel_id=1, source_target_pairs={{0,1},{1,0},{2,3},{3,2},{4,5},{5,4},{6,7},{7,6},{8,9},{9,8},{10,11... | collective-permute-start | bytes 1572872 | tf_op jit(solution)/shard_map/ppermute | solution.py:392
  280.8 20.0 %collective-permute-start.3 = (bf16[256,1024]{1,0:T(8,128)(2,1)}, bf16[256,1024]{1,0:T(8,128)(2,1)S(1)}, u32[]{:S(2)}, u32[]{:S(2)}) collective-permute-start(bf16[256,1024]{1,0:T(8,128)(2,1)} %select_convert_fusion.2), channel_id=1, source_target_pairs={{0,1},{1,0},{2,3},{3,2},{4,5},{5,4},{6,7},{7,6},{8,9},{9,8},{10,11... | collective-permute-start | bytes 1572872 | tf_op jit(solution)/shard_map/ppermute | solution.py:392
  281.4 3.9 copy-start.22
  281.5 3.9 copy-start.24
  281.5 3.9 copy-start.26
  281.5 12.1 %copy-start.40 = (f32[1024]{0:T(1024)S(1)}, f32[1024]{0:T(1024)}, u32[]{:S(2)}) copy-start(f32[1024]{0:T(1024)} %copy-done.39) | copy-start | bytes 12292
  281.5 12.1 %copy-start.45 = (f32[256]{0:T(256)S(1)}, f32[256]{0:T(256)}, u32[]{:S(2)}) copy-start(f32[256]{0:T(256)} %copy-done.44) | copy-start | bytes 3076
  285.3 8.2 %copy-start.12 = (f32[512,1024]{1,0:T(8,128)S(1)}, f32[512,1024]{1,0:T(8,128)}, u32[]{:S(2)}) copy-start(f32[512,1024]{1,0:T(8,128)} %copy-done.11) | copy-start | bytes 6291460
  285.3 10.6 %copy-start.54 = (f32[64]{0:T(128)S(1)}, f32[64]{0:T(128)}, u32[]{:S(2)}) copy-start(f32[64]{0:T(128)} %get-tuple-element.61) | copy-start | bytes 772
  285.4 15.5 %copy-start.4 = (f32[256,1024]{1,0:T(8,128)S(1)}, f32[256,1024]{1,0:T(8,128)}, u32[]{:S(2)}) copy-start(f32[256,1024]{1,0:T(8,128)} %copy-done.3) | copy-start | bytes 3145732
  296.0 8.6 %collective-permute-start.8 = (f32[1,2176]{1,0:T(1,128)S(1)}, f32[1,2176]{1,0:T(1,128)S(1)}, u32[]{:S(2)}, u32[]{:S(2)}) collective-permute-start(f32[1,2176]{1,0:T(1,128)S(1)} %broadcast_in_dim.31), channel_id=1, source_target_pairs={{0,1},{1,0},{2,3},{3,2},{4,5},{5,4},{6,7},{7,6},{8,9},{9,8},{10,11... | collective-permute-start | bytes 26120 | tf_op jit(solution)/shard_map/ppermute | solution.py:392
  409.9 8.5 %copy-start.20 = (f32[64,2304]{1,0:T(8,128)S(1)}, f32[64,2304]{1,0:T(8,128)}, u32[]{:S(2)}) copy-start(f32[64,2304]{1,0:T(8,128)} %get-tuple-element.20) | copy-start | bytes 1769476
  (8 other events, 13.5 us)

commit v2 on v1

--- a/solution.py
+++ b/solution.py
@@ -184,15 +184,17 @@
                 else:
                     event()
             if s:
-                side(s - 1, act)
-        side(length - 1, act)
-
-    def side(s, act):
+                side(s - 1, act, range(1, count))
+            else:
+                side(0, act, (0,))
+        side(length - 1, act, range(1, count))
+
+    def side(s, act, chosen):
         for sign in (1, -1) if s else (0,):
             oz = z - s * sign
 
             def event(oz=oz):
-                for k in range(count):
+                for k in chosen:
                     act(k, oz, None, 0)
 
             if s:
@@ -201,6 +203,15 @@
                 event()
 
     def begin(k, oz, s, sign):
+        if k == 0 and s != 0:
+            for ox in (1 - x,) if s is None else (x, 1 - x):
+                arrived(k, at.device(oz, ox, c))
+                if sign >= 0:
+                    pl.when(z < length - 1)(lambda: move(k, oz, ox, 0, above, False).start())
+                if sign <= 0:
+                    pl.when(z > 0)(lambda: move(k, oz, ox, 1, below, False).start())
+                move(k, oz, ox, 3, sibling, False).start()
+            return
         if s is None:
             arrived(k, at.device(oz, 1 - x, c))
             move(k, oz, 1 - x, 3, sibling, False).start()
@@ -216,6 +227,14 @@
         move(k, oz, x, 3, sibling, first).start()
 
     def finish(k, oz, s, sign):
+        if k == 0 and s != 0:
+            for ox in (1 - x,) if s is None else (x, 1 - x):
+                if sign >= 0:
+                    pl.when(z < length - 1)(lambda: move(k, oz, ox, 0, above, False).wait_send())
+                if sign <= 0:
+                    pl.when(z > 0)(lambda: move(k, oz, ox, 1, below, False).wait_send())
+                move(k, oz, ox, 3, sibling, False).wait_send()
+            return
         if s is None:
             move(k, oz, 1 - x, 3, sibling, False).wait_send()
             return

time: 428 us -> 432 us (level)
    pallas_call x1, Pallas kernels: 103 us -> 108 us  [gather_rows(): pl.pallas_call(functools.partial(gather_kernel, dp, count, rows), out_sha...]
where the time goes in v2:
time: 432 us; the launch traced here: 424 us
  Pallas kernels  209 us (48%)
  matrix products  73.8 us (17%)
  waiting for transfers between devices  43.3 us (10%)
  other arithmetic  42.3 us (10%)
  local copies, waits for them, and re-layouts  41.6 us (10%)
  starting transfers between devices  12 us (3%)
    pallas_call x1, Pallas kernels, gather_rows(): pl.pallas_call(functools.partial(gather_kernel, dp, count, rows), out_sha...  108 us
    pallas_call x1, Pallas kernels, scatter_rows(): pl.pallas_call(functools.partial(scatter_kernel, dp, count, rows), out_sh...  101 us
    ppermute x9, waiting for transfers between devices, exchange(): return lax.ppermute(values, 'tensor', ((0, 1), (1, 0)))  43.3 us
    dot_general x8, matrix products, contract(): lax.dot_general(left, right, (((left_dim,), (right_dim,)), ((), ())), pre...  34.3 us
    dot_general x4, matrix products, fdot(): return jnp.dot(left, right, preferred_element_type=jnp.float32)  26.2 us
    ppermute x9, starting transfers between devices, exchange(): return lax.ppermute(values, 'tensor', ((0, 1), (1, 0)))  12 us
  transfers between devices with their start and end apart: 9, of which 7 were waited for; matrix products, arithmetic and copies ran while one was open for 11% of the time, Pallas kernels for 0%

profile of v2, /device:TPU:0, one launch (start us, length us, event | category | flops | bytes accessed | tf_op | source)
XLA Modules:
  0.0 424.2 jit_solution(1342975100778162772)
XLA Ops:
  0.7 1.3 fusion.41
  5.1 1.1 slice_bitcast_fusion.3
  8.0 107.8 %gather_rows.1 = (bf16[1024,1664]{1,0:T(8,128)(2,1)}, bf16[1024,4608]{1,0:T(8,128)(2,1)}, bf16[1024,2304]{1,0:T(8,128)(2,1)}) custom-call(bf16[64,1664]{1,0:T(8,128)(2,1)} %copy-done.31, bf16[64,4608]{1,0:T(8,128)(2,1)} %pad_maximum_fusion.18.refs_1_, bf16[64,2304]{1,0:T(8,128)(2,1)} %bitcast.185), custom_call_target="tpu_custom_call" | custom-call | tf_op jit(solution)/shard_map/gather_rows/pallas_call | solution.py:261
  117.9 1.6 collective-permute-start
  120.9 11.4 %collective-permute-done = bf16[256,1024]{1,0:T(8,128)(2,1)S(1)} collective-permute-done((bf16[256,1024]{1,0:T(8,128)(2,1)S(1)}, bf16[256,1024]{1,0:T(8,128)(2,1)S(1)}, u32[]{:S(2)}, u32[]{:S(2)}) %collective-permute-start) | collective-permute-done | bytes 524320 | tf_op jit(solution)/shard_map/ppermute | solution.py:411
  132.7 3.2 fusion.19
  138.8 1.2 copy.106
  141.2 1.6 copy.109
  144.1 1.5 fusion.81
  145.7 1.5 fusion.4
  147.2 1.8 copy-done
  149.0 2.7 fusion.21
  151.8 2.2 fusion.53
  154.0 1.6 collective-permute-start.1
  156.1 12.8 %collective-permute-done.1 = bf16[256,1024]{1,0:T(8,128)(2,1)S(1)} collective-permute-done((bf16[256,1024]{1,0:T(8,128)(2,1)S(1)}, bf16[256,1024]{1,0:T(8,128)(2,1)S(1)}, u32[]{:S(2)}, u32[]{:S(2)}) %collective-permute-start.1) | collective-permute-done | bytes 524320 | tf_op jit(solution)/shard_map/ppermute | solution.py:411
  170.2 1.5 collective-permute-start.2
  171.7 1.1 mul.635
  172.8 2.5 copy.114
  175.4 1.2 mul.640
  176.6 1.3 mul.641
  177.9 1.1 mul.631
  179.0 2.5 copy.119
  182.3 1.3 broadcast_select_fusion.3
  183.6 6.6 %collective-permute-done.2 = bf16[256,1024]{1,0:T(8,128)(2,1)} collective-permute-done((bf16[256,1024]{1,0:T(8,128)(2,1)}, bf16[256,1024]{1,0:T(8,128)(2,1)}, u32[]{:S(2)}, u32[]{:S(2)}) %collective-permute-start.2) | collective-permute-done | bytes 524320 | tf_op jit(solution)/shard_map/ppermute | solution.py:411
  190.2 1.5 broadcast_select_fusion.5
  191.7 11.7 %fusion.56 = f32[512,4608]{1,0:T(8,128)} fusion(bf16[1024,4608]{1,0:T(8,128)(2,1)} %get-tuple-element.16, bf16[256,1024]{1,0:T(8,128)(2,1)S(1)} %get-tuple-element.88, bf16[256,1024]{1,0:T(8,128)(2,1)S(1)} %get-tuple-element.87), kind=kOutput, calls=%fused_computation.100 | convolution fusion | flops 4833935360 | bytes 19922944 | tf_op jit(solution)/shard_map/dot_general | solution.py:60
  203.4 8.9 %multiply_convert_fusion.1 = (bf16[512,2304]{1,0:T(8,128)(2,1)}, bf16[512,2304]{1,0:T(8,128)(2,1)}, bf16[512,2304]{1,0:T(8,128)(2,1)}) fusion(f32[512,4608]{1,0:T(8,128)} %fusion.56, bf16[1024,2304]{1,0:T(8,128)(2,1)S(1)} %bitcast.209, bf16[256,1024]{1,0:T(8,128)(2,1)S(1)} %get-tuple-element.86, bf16[256,1024]{1,0:T(8,128)(2,1)S(1)} %get-tuple-element.85), kind=kOutput, calls=%fused_computation.18 | convolution fusion | flops 2435710976 | bytes 22282240 | tf_op jit(solution)/shard_map/dot_general | solution.py:60
  212.3 6.9 %fusion.16 = f32[512,1024]{1,0:T(8,128)S(1)} fusion(bf16[1024,4608]{1,0:T(8,128)(2,1)S(1)} %bitcast.207, bf16[512,2304]{1,0:T(8,128)(2,1)} %get-tuple-element.71, bf16[512,2304]{1,0:T(8,128)(2,1)} %get-tuple-element.70), kind=kOutput, calls=%fused_computation.29 | convolution fusion | flops 4841275392 | bytes 16252928 | tf_op jit(solution)/shard_map/dot_general | solution.py:54
  219.3 1.6 collective-permute-start.5
  220.9 10.0 %convolution_convert_fusion.refs_1_ = bf16[1024,4608]{1,0:T(8,128)(2,1)} fusion(bf16[512,2304]{1,0:T(8,128)(2,1)} %get-tuple-element.71, bf16[512,2304]{1,0:T(8,128)(2,1)} %get-tuple-element.70, bf16[256,1024]{1,0:T(8,128)(2,1)S(1)} %get-tuple-element.88, bf16[256,1024]{1,0:T(8,128)(2,1)S(1)} %get-tuple-element.87), kind=kOutput, calls=%fused_computation | convolution fusion | flops 4848091136 | bytes 15204352 | tf_op jit(solution)/shard_map/dot_general | solution.py:54
  232.6 1.8 fusion.77
  234.4 1.6 collective-permute-start.6
  235.9 4.0 fusion.82
  239.9 4.3 %convolution_convert_fusion.1.refs_2_ = bf16[1024,2304]{1,0:T(8,128)(2,1)} fusion(bf16[512,2304]{1,0:T(8,128)(2,1)S(1)} %copy-done.55, bf16[256,1024]{1,0:T(8,128)(2,1)S(1)} %get-tuple-element.86, bf16[256,1024]{1,0:T(8,128)(2,1)S(1)} %get-tuple-element.85), kind=kOutput, calls=%fused_computation.14 | convolution fusion | flops 2420375552 | bytes 8126464 | tf_op jit(solution)/shard_map/dot_general | solution.py:54
  244.3 1.9 collective-permute-done.6
  246.3 2.4 convolution_convert_fusion.4
  248.7 2.3 fusion.29
  251.0 2.7 fusion
  253.7 2.8 fusion.9
  256.6 2.3 broadcast_multiply_fusion
  258.9 1.8 fusion.83
  260.7 1.8 copy.123
  263.6 1.9 multiply_reduce_fusion.5
  266.4 1.1 copy.122
  267.5 1.5 bitcast_multiply_fusion.2
  269.1 1.2 pad_maximum_fusion.8
  270.4 2.5 copy.115
  272.9 2.5 copy.113
  275.6 1.3 copy.118
  276.9 3.8 multiply_reduce_fusion
  280.8 1.3 fusion.17
  283.0 1.5 collective-permute-start.7
  286.1 3.8 convolution_convert_fusion.2
  290.0 1.7 convolution_convert_fusion.3
  291.7 6.4 %collective-permute-done.7 = bf16[256,1024]{1,0:T(8,128)(2,1)} collective-permute-done((bf16[256,1024]{1,0:T(8,128)(2,1)}, bf16[256,1024]{1,0:T(8,128)(2,1)}, u32[]{:S(2)}, u32[]{:S(2)}) %collective-permute-start.7) | collective-permute-done | bytes 524320 | tf_op jit(solution)/shard_map/ppermute | solution.py:411
  298.2 2.4 fusion.44
  300.6 1.6 collective-permute-start.8
  302.2 3.3 collective-permute-done.3
  305.5 3.8 fusion.36
  309.8 3.2 fusion.15.refs_0_
  313.1 101.3 %scatter_rows.1 = (f32[64,1664]{1,0:T(8,128)}, f32[64,4608]{1,0:T(8,128)}, f32[64,2304]{1,0:T(8,128)}) custom-call(bf16[1024,1664]{1,0:T(8,128)(2,1)} %fusion.15.refs_0_, bf16[1024,4608]{1,0:T(8,128)(2,1)} %convolution_convert_fusion.refs_1_, bf16[1024,2304]{1,0:T(8,128)(2,1)} %convolution_convert_fusion.1.refs_2_), custom_call_target="tpu_custom_call" | custom-call | tf_op jit(solution)/shard_map/scatter_rows/pallas_call | solution.py:391
  416.0 1.7 slice_bitcast_fusion.5
  419.8 1.3 slice_bitcast_fusion.1
  421.8 1.1 pad_maximum_fusion.3
  (208 shorter events, 29.0 us)
Async XLA Ops:
  0.6 117.1 %copy-start.1 = (bf16[256,1024]{1,0:T(8,128)(2,1)S(1)}, bf16[256,1024]{1,0:T(8,128)(2,1)}, u32[]{:S(2)}) copy-start(bf16[256,1024]{1,0:T(8,128)(2,1)} %param.11) | copy-start | bytes 1572868
  0.7 119.1 %copy-start.53 = (s32[1,512]{1,0:T(1,128)S(1)}, s32[1,512]{1,0:T(1,128)}, u32[]{:S(2)}) copy-start(s32[1,512]{1,0:T(1,128)} %param.14) | copy-start | bytes 6148
  0.7 120.0 %copy-start.51 = (s32[1,512]{1,0:T(1,128)S(1)}, s32[1,512]{1,0:T(1,128)}, u32[]{:S(2)}) copy-start(s32[1,512]{1,0:T(1,128)} %param.13) | copy-start | bytes 6148
  2.0 130.7 %copy-start.44 = (f32[256]{0:T(256)}, f32[256]{0:T(256)S(1)}, u32[]{:S(2)}) copy-start(f32[256]{0:T(256)S(1)} %add_rsqrt_fusion.3) | copy-start | bytes 3076
  117.7 14.9 %copy-start.39 = (f32[1024]{0:T(1024)}, f32[1024]{0:T(1024)S(1)}, u32[]{:S(2)}) copy-start(f32[1024]{0:T(1024)S(1)} %get-tuple-element.64) | copy-start | bytes 12292
  117.9 14.4 %collective-permute-start = (bf16[256,1024]{1,0:T(8,128)(2,1)S(1)}, bf16[256,1024]{1,0:T(8,128)(2,1)S(1)}, u32[]{:S(2)}, u32[]{:S(2)}) collective-permute-start(bf16[256,1024]{1,0:T(8,128)(2,1)S(1)} %fusion.32), channel_id=1, source_target_pairs={{0,1},{1,0},{2,3},{3,2},{4,5},{5,4},{6,7},{7,6},{8,9},{9,8},{10,11... | collective-permute-start | bytes 1572872 | tf_op jit(solution)/shard_map/ppermute | solution.py:411
  119.7 20.4 %copy-start.48 = (f32[64,1]{0,1:T(1,128)}, f32[64,1]{0,1:T(1,128)S(1)}, u32[]{:S(2)}) copy-start(f32[64,1]{0,1:T(1,128)S(1)} %copy.142) | copy-start | bytes 772
  120.7 23.0 %copy-start.7 = (f32[512,64]{0,1:T(8,128)}, f32[512,64]{0,1:T(8,128)S(1)}, u32[]{:S(2)}) copy-start(f32[512,64]{0,1:T(8,128)S(1)} %get-tuple-element.104) | copy-start | bytes 393220
  132.6 3.3 copy-start.27
  132.6 3.3 copy-start.29
  138.8 4.2 copy-start.46
  140.2 3.2 copy-start.34
  140.3 3.1 copy-start.49
  145.6 3.4 copy-start
  145.6 3.4 copy-start.38
  145.7 3.4 copy-start.16
  147.2 4.6 %copy-start.41 = (f32[4,2,512]{2,1,0:T(2,128)}, f32[4,2,512]{2,1,0:T(2,128)S(1)}, u32[]{:S(2)}) copy-start(f32[4,2,512]{2,1,0:T(2,128)S(1)} %fusion.4) | copy-start | bytes 49156
  151.7 4.4 %copy-start.21 = (bf16[4,64,2,512]{3,1,2,0:T(8,128)(2,1)}, bf16[4,64,2,512]{3,1,2,0:T(8,128)(2,1)S(1)}, u32[]{:S(2)}) copy-start(bf16[4,64,2,512]{3,1,2,0:T(8,128)(2,1)S(1)} %fusion.21) | copy-start | bytes 1572868
  151.8 17.5 %copy-start.36 = (f32[1024]{0:T(1024)S(1)}, f32[1024]{0:T(1024)}, u32[]{:S(2)}) copy-start(f32[1024]{0:T(1024)} %get-tuple-element.63) | copy-start | bytes 12292
  154.0 14.9 %collective-permute-start.1 = (bf16[256,1024]{1,0:T(8,128)(2,1)S(1)}, bf16[256,1024]{1,0:T(8,128)(2,1)S(1)}, u32[]{:S(2)}, u32[]{:S(2)}) collective-permute-start(bf16[256,1024]{1,0:T(8,128)(2,1)S(1)} %select_convert_fusion.3), channel_id=1, source_target_pairs={{0,1},{1,0},{2,3},{3,2},{4,5},{5,4},{6,7},{7,6},{8,9},{9,8},{10,11... | collective-permute-start | bytes 1572872 | tf_op jit(solution)/shard_map/ppermute | solution.py:411
  155.6 26.7 %collective-permute-start.4 = (bf16[256,1024]{1,0:T(8,128)(2,1)}, bf16[256,1024]{1,0:T(8,128)(2,1)}, u32[]{:S(2)}, u32[]{:S(2)}) collective-permute-start(bf16[256,1024]{1,0:T(8,128)(2,1)} %param.12), channel_id=1, source_target_pairs={{0,1},{1,0},{2,3},{3,2},{4,5},{5,4},{6,7},{7,6},{8,9},{9,8},{10,11... | collective-permute-start | bytes 1572872 | tf_op jit(solution)/shard_map/ppermute | solution.py:411
  170.2 19.9 %collective-permute-start.2 = (bf16[256,1024]{1,0:T(8,128)(2,1)}, bf16[256,1024]{1,0:T(8,128)(2,1)}, u32[]{:S(2)}, u32[]{:S(2)}) collective-permute-start(bf16[256,1024]{1,0:T(8,128)(2,1)} %multiply_convert_fusion.3), channel_id=1, source_target_pairs={{0,1},{1,0},{2,3},{3,2},{4,5},{5,4},{6,7},{7,6},{8,9},{9,8},{10,11... | collective-permute-start | bytes 1572872 | tf_op jit(solution)/shard_map/ppermute | solution.py:411
  179.0 11.1 %copy-start.37 = (f32[1024]{0:T(1024)S(1)}, f32[1024]{0:T(1024)}, u32[]{:S(2)}) copy-start(f32[1024]{0:T(1024)} %get-tuple-element.63) | copy-start | bytes 12292
  179.0 11.1 %copy-start.43 = (f32[256]{0:T(256)S(1)}, f32[256]{0:T(256)}, u32[]{:S(2)}) copy-start(f32[256]{0:T(256)} %copy-done.42) | copy-start | bytes 3076
  190.2 13.2 %slice-start.5 = ((s8[4718592]{0:T(1024)(128)(4,1)}), s8[4194304]{0:T(1024)(128)(4,1)S(1)}, s32[]{:S(2)}) async-start(s8[4718592]{0:T(1024)(128)(4,1)} %bitcast.208), calls=%async_computation.5 | async-start | bytes 8388608
  191.6 11.7 %slice-start.6 = ((s8[4718592]{0:T(1024)(128)(4,1)}), s8[524288]{0:T(1024)(128)(4,1)S(1)}, s32[]{:S(2)}) async-start(s8[4718592]{0:T(1024)(128)(4,1)} %bitcast.208), calls=%async_computation.6 | async-start | bytes 1048576
  191.7 20.6 %slice-start.2 = ((s8[9437184]{0:T(1024)(128)(4,1)}), s8[4194304]{0:T(1024)(128)(4,1)S(1)}, s32[]{:S(2)}) async-start(s8[9437184]{0:T(1024)(128)(4,1)} %bitcast.206), calls=%async_computation.2 | async-start | bytes 8388608
  203.4 8.9 %slice-start.3 = ((s8[9437184]{0:T(1024)(128)(4,1)}), s8[4194304]{0:T(1024)(128)(4,1)S(1)}, s32[]{:S(2)}) async-start(s8[9437184]{0:T(1024)(128)(4,1)} %bitcast.206), calls=%async_computation.3 | async-start | bytes 8388608
  203.4 8.9 %slice-start.4 = ((s8[9437184]{0:T(1024)(128)(4,1)}), s8[1048576]{0:T(1024)(128)(4,1)S(1)}, s32[]{:S(2)}) async-start(s8[9437184]{0:T(1024)(128)(4,1)} %bitcast.206), calls=%async_computation.4 | async-start | bytes 2097152
  219.3 12.7 %collective-permute-start.5 = (bf16[256,1024]{1,0:T(8,128)(2,1)S(1)}, bf16[256,1024]{1,0:T(8,128)(2,1)S(1)}, u32[]{:S(2)}, u32[]{:S(2)}) collective-permute-start(bf16[256,1024]{1,0:T(8,128)(2,1)S(1)} %select_convert_fusion.1), channel_id=1, source_target_pairs={{0,1},{1,0},{2,3},{3,2},{4,5},{5,4},{6,7},{7,6},{8,9},{9,8},{10,11... | collective-permute-start | bytes 1572872 | tf_op jit(solution)/shard_map/ppermute | solution.py:411
  231.0 4.9 %copy-start.55 = (bf16[512,2304]{1,0:T(8,128)(2,1)S(1)}, bf16[512,2304]{1,0:T(8,128)(2,1)}, u32[]{:S(2)}) copy-start(bf16[512,2304]{1,0:T(8,128)(2,1)} %get-tuple-element.72) | copy-start | bytes 7077892
  232.5 3.4 copy-start.3
  234.4 11.8 %collective-permute-start.6 = (bf16[256,1024]{1,0:T(8,128)(2,1)S(1)}, bf16[256,1024]{1,0:T(8,128)(2,1)S(1)}, u32[]{:S(2)}, u32[]{:S(2)}) collective-permute-start(bf16[256,1024]{1,0:T(8,128)(2,1)S(1)} %fusion.77), channel_id=1, source_target_pairs={{0,1},{1,0},{2,3},{3,2},{4,5},{5,4},{6,7},{7,6},{8,9},{9,8},{10,11... | collective-permute-start | bytes 1572872 | tf_op jit(solution)/shard_map/ppermute | solution.py:411
  235.9 12.7 %slice-start = ((s8[8388608]{0:T(1024)(128)(4,1)}), s8[4194304]{0:T(1024)(128)(4,1)S(1)}, s32[]{:S(2)}) async-start(s8[8388608]{0:T(1024)(128)(4,1)} %bitcast.160), calls=%async_computation | async-start | bytes 8388608
  239.9 8.7 %slice-start.1 = ((s8[8388608]{0:T(1024)(128)(4,1)}), s8[4194304]{0:T(1024)(128)(4,1)S(1)}, s32[]{:S(2)}) async-start(s8[8388608]{0:T(1024)(128)(4,1)} %bitcast.160), calls=%async_computation.1 | async-start | bytes 8388608
  246.2 4.7 %copy-start.23 = (bf16[256,1024]{1,0:T(8,128)(2,1)}, bf16[256,1024]{1,0:T(8,128)(2,1)S(1)}, u32[]{:S(2)}) copy-start(bf16[256,1024]{1,0:T(8,128)(2,1)S(1)} %get-tuple-element.83) | copy-start | bytes 1572868
  246.2 4.7 %copy-start.25 = (bf16[256,1024]{1,0:T(8,128)(2,1)}, bf16[256,1024]{1,0:T(8,128)(2,1)S(1)}, u32[]{:S(2)}) copy-start(bf16[256,1024]{1,0:T(8,128)(2,1)S(1)} %get-tuple-element.84) | copy-start | bytes 1572868
  248.7 2.3 copy-start.17
  253.6 2.9 copy-start.6
  253.7 2.9 copy-start.8
  256.5 2.4 copy-start.15
  258.9 4.7 %copy-start.35 = (f32[512,4]{0,1:T(4,128)S(1)}, f32[512,4]{0,1:T(4,128)}, u32[]{:S(2)}) copy-start(f32[512,4]{0,1:T(4,128)} %copy-done.34) | copy-start | bytes 24580
  258.9 4.7 %copy-start.50 = (f32[64,1]{0,1:T(1,128)S(1)}, f32[64,1]{0,1:T(1,128)}, u32[]{:S(2)}) copy-start(f32[64,1]{0,1:T(1,128)} %copy-done.48) | copy-start | bytes 772
  260.7 6.8 %copy-start.9 = (f32[512,64]{0,1:T(8,128)S(1)}, f32[512,64]{0,1:T(8,128)}, u32[]{:S(2)}) copy-start(f32[512,64]{0,1:T(8,128)} %copy-done.7) | copy-start | bytes 393220
  263.6 5.4 %copy-start.47 = (f32[64,1]{0,1:T(1,128)S(1)}, f32[64,1]{0,1:T(1,128)}, u32[]{:S(2)}) copy-start(f32[64,1]{0,1:T(1,128)} %copy.143) | copy-start | bytes 772
  267.5 13.2 %copy-start.33 = (bf16[512,256]{1,0:T(8,128)(2,1)}, bf16[512,256]{1,0:T(8,128)(2,1)S(1)}, u32[]{:S(2)}) copy-start(bf16[512,256]{1,0:T(8,128)(2,1)S(1)} %copy.122) | copy-start | bytes 786436
  270.4 6.5 %copy-start.52 = (f32[512]{0:T(512)S(1)}, f32[512]{0:T(512)}, u32[]{:S(2)}) copy-start(f32[512]{0:T(512)} %mul.641) | copy-start | bytes 6148
  275.6 5.1 %copy-start.32 = (bf16[512,256]{1,0:T(8,128)(2,1)S(1)}, bf16[512,256]{1,0:T(8,128)(2,1)}, u32[]{:S(2)}) copy-start(bf16[512,256]{1,0:T(8,128)(2,1)} %copy.123) | copy-start | bytes 786436
  276.9 3.8 copy-start.30
  280.8 3.8 copy-start.10
  280.8 5.3 %copy-start.28 = (bf16[256,1024]{1,0:T(8,128)(2,1)S(1)}, bf16[256,1024]{1,0:T(8,128)(2,1)}, u32[]{:S(2)}) copy-start(bf16[256,1024]{1,0:T(8,128)(2,1)} %copy-done.27) | copy-start | bytes 1572868
  282.0 3.4 copy-start.11
  283.0 15.1 %collective-permute-start.7 = (bf16[256,1024]{1,0:T(8,128)(2,1)}, bf16[256,1024]{1,0:T(8,128)(2,1)}, u32[]{:S(2)}, u32[]{:S(2)}) collective-permute-start(bf16[256,1024]{1,0:T(8,128)(2,1)} %select_convert_fusion), channel_id=1, source_target_pairs={{0,1},{1,0},{2,3},{3,2},{4,5},{5,4},{6,7},{7,6},{8,9},{9,8},{10,11... | collective-permute-start | bytes 1572872 | tf_op jit(solution)/shard_map/ppermute | solution.py:411
  285.4 20.0 %collective-permute-start.3 = (bf16[256,1024]{1,0:T(8,128)(2,1)}, bf16[256,1024]{1,0:T(8,128)(2,1)S(1)}, u32[]{:S(2)}, u32[]{:S(2)}) collective-permute-start(bf16[256,1024]{1,0:T(8,128)(2,1)} %select_convert_fusion.2), channel_id=1, source_target_pairs={{0,1},{1,0},{2,3},{3,2},{4,5},{5,4},{6,7},{7,6},{8,9},{9,8},{10,11... | collective-permute-start | bytes 1572872 | tf_op jit(solution)/shard_map/ppermute | solution.py:411
  286.1 3.9 copy-start.22
  286.1 3.9 copy-start.24
  286.1 3.9 copy-start.26
  286.1 12.1 %copy-start.40 = (f32[1024]{0:T(1024)S(1)}, f32[1024]{0:T(1024)}, u32[]{:S(2)}) copy-start(f32[1024]{0:T(1024)} %copy-done.39) | copy-start | bytes 12292
  286.1 12.1 %copy-start.45 = (f32[256]{0:T(256)S(1)}, f32[256]{0:T(256)}, u32[]{:S(2)}) copy-start(f32[256]{0:T(256)} %copy-done.44) | copy-start | bytes 3076
  289.9 8.2 %copy-start.12 = (f32[512,1024]{1,0:T(8,128)S(1)}, f32[512,1024]{1,0:T(8,128)}, u32[]{:S(2)}) copy-start(f32[512,1024]{1,0:T(8,128)} %copy-done.11) | copy-start | bytes 6291460
  290.0 10.6 %copy-start.54 = (f32[64]{0:T(128)S(1)}, f32[64]{0:T(128)}, u32[]{:S(2)}) copy-start(f32[64]{0:T(128)} %get-tuple-element.61) | copy-start | bytes 772
  290.0 15.5 %copy-start.4 = (f32[256,1024]{1,0:T(8,128)S(1)}, f32[256,1024]{1,0:T(8,128)}, u32[]{:S(2)}) copy-start(f32[256,1024]{1,0:T(8,128)} %copy-done.3) | copy-start | bytes 3145732
  300.6 8.7 %collective-permute-start.8 = (f32[1,2176]{1,0:T(1,128)S(1)}, f32[1,2176]{1,0:T(1,128)S(1)}, u32[]{:S(2)}, u32[]{:S(2)}) collective-permute-start(f32[1,2176]{1,0:T(1,128)S(1)} %broadcast_in_dim.31), channel_id=1, source_target_pairs={{0,1},{1,0},{2,3},{3,2},{4,5},{5,4},{6,7},{7,6},{8,9},{9,8},{10,11... | collective-permute-start | bytes 26120 | tf_op jit(solution)/shard_map/ppermute | solution.py:411
  414.4 8.5 %copy-start.20 = (f32[64,2304]{1,0:T(8,128)S(1)}, f32[64,2304]{1,0:T(8,128)}, u32[]{:S(2)}) copy-start(f32[64,2304]{1,0:T(8,128)} %get-tuple-element.20) | copy-start | bytes 1769476
  (8 other events, 13.5 us)
